TPU v7x, 256 devices: a whole 4x4x8 slice. The times are simulated.
256 devices in a mesh: pool: 2 (over core), seq: 16 (over x, y), head: 8 (over z).
Axes of the slice: x: 4, y: 4, z: 8, core: 2. Of those that a mesh axis runs over, the one named last changes fastest.
Arguments:
- x_in: bfloat16 [1, 16384, 8, 2048], P(None, 'seq', 'head', 'pool'), may hold values from -6 to 6
- gate_in: bfloat16 [1, 16384, 8, 2048], P(None, 'seq', 'head', 'pool'), may hold values from -6 to 6
- dt_raw: bfloat16 [1, 16384, 8, 32], P(None, 'seq', 'head', 'pool'), may hold values from -4 to 4
- b_in: bfloat16 [1, 16384, 8, 256], P(None, 'seq', 'head'), may hold values from -0.375 to 0.375
- c_in: bfloat16 [1, 16384, 8, 256], P(None, 'seq', 'head'), may hold values from -6 to 6
- lengths: int32 [1], replicated, may hold values from 4096 to 16384
- decay_rate: float32 [8, 32], P('head', 'pool'), may hold values from 0.0001 to 0.05
- skip_gain: float32 [8, 32], P('head', 'pool'), may hold values from 0.5 to 2
- norm_gain: float32 [8, 2048], P('head', 'pool'), may hold values from 0.5 to 1.5
- dec_states: float32 [64, 8, 32, 64, 256], P('seq', 'head', 'pool'), may hold values from -18 to 18
- dec_x: bfloat16 [8, 64, 8, 2048], P(None, 'seq', 'head', 'pool'), may hold values from -6 to 6
- dec_gate: bfloat16 [8, 64, 8, 2048], P(None, 'seq', 'head', 'pool'), may hold values from -6 to 6
- dec_dt: bfloat16 [8, 64, 8, 32], P(None, 'seq', 'head', 'pool'), may hold values from -4 to 4
- dec_b: bfloat16 [8, 64, 8, 256], P(None, 'seq', 'head'), may hold values from -0.375 to 0.375
- dec_c: bfloat16 [8, 64, 8, 256], P(None, 'seq', 'head'), may hold values from -6 to 6
- slots: int32 [64], P('seq'), may hold values from -1 to 0, as said below
Outputs:
- prefill_out: bfloat16 [1, 16384, 8, 2048], P(None, 'seq', 'head', 'pool')
- decode_out: bfloat16 [8, 64, 8, 2048], P(None, 'seq', 'head', 'pool')
Inputs may be any that keep to these rules, and one draw needn't show every extreme that they name: `lengths`: valid positions of each prompt; later positions are padding. `slots`: each aligned block of 4 decode sequences holds at least one that continues a prompt and at least one that keeps its own state.
All inputs are finite; a program needn't handle non-finite values.
Results may differ from a plain program's by a relative error of at most 0.001.
Values sent between devices are 32-bit elements; how exact they have to be, the bound alone decides.
No kernel may reach another device: no remote copies, remote signals or barrier semaphores. Data moves between devices by JAX's collectives and lax.ppermute only.
A program may use at most 128 MiB of HBM per device.

v0:
```python
import jax
import jax.numpy as jnp
from jax import lax
from jax.experimental import pallas as pl
from jax.experimental.pallas import tpu as pltpu
from jax.sharding import Mesh
from jax.sharding import PartitionSpec as P

SEQ = ("seq_0", "seq_1")
HEAD_DIM = 64
SPAN = 256
TILE = 128
EPS = 1e-05
F32 = jnp.float32
BF16 = jnp.bfloat16


def iota(shape, dim):
    return lax.broadcasted_iota(jnp.int32, shape, dim)


def dot(a, b, ca, cb):
    return lax.dot_general(a, b, (((ca,), (cb,)), ((), ())), preferred_element_type=F32)


def exact_dot(a, b):
    return jnp.dot(a, b, precision=lax.Precision.HIGHEST, preferred_element_type=F32)


def split2(v):
    hi = v.astype(BF16)
    return hi, (v - hi.astype(F32)).astype(BF16)


def split3(v):
    hi = v.astype(BF16)
    rest = v - hi.astype(F32)
    mid = rest.astype(BF16)
    low = (rest - mid.astype(F32)).astype(BF16)
    return jnp.concatenate([hi, mid, low], axis=0)


def spread(heads, width):
    one = iota((heads, width), 0) == iota((heads, width), 1) // HEAD_DIM
    return jnp.where(one, 1.0, 0.0)


def spread3(heads, width):
    one = spread(heads, width).astype(BF16)
    return jnp.concatenate([one, one, one], axis=0)


def per_channel(v, table):
    return dot(split3(v), table, 0, 0)


def as_column(row):
    n = row.shape[1]
    return jnp.sum(jnp.where(iota((n, n), 0) == iota((n, n), 1), row, 0.0), axis=1, keepdims=True)


def as_row(column, width):
    n = column.shape[0]
    same = iota((n, width), 0) == iota((n, width), 1)
    return jnp.sum(jnp.where(same, column, 0.0), axis=0, keepdims=True)


def silu(v):
    return v * jax.nn.sigmoid(v)


def head_terms(dt_ref, rate, first, limit):
    heads, span = dt_ref.shape
    live = first + iota((heads, span), 1) < limit
    step = jnp.where(live, jax.nn.softplus(dt_ref[...].astype(F32)), 0.0)
    upper = jnp.where(iota((span, span), 0) <= iota((span, span), 1), 1.0, 0.0).astype(BF16)
    sums = dot(split3(-step * rate), upper, 1, 0)
    return step, sums[:heads] + sums[heads : 2 * heads] + sums[2 * heads :]


def state_kernel(limit_ref, rate_ref, dt_ref, x_ref, b_ref, dec_c_ref, out_ref, state, total):
    t = pl.program_id(0)
    heads, span = dt_ref.shape
    width = x_ref.shape[1]

    @pl.when(t == 0)
    def _():
        state[...] = jnp.zeros_like(state)
        total[...] = jnp.zeros_like(total)

    table = spread3(heads, width)
    step, cum = head_terms(dt_ref, as_column(rate_ref[...]), t * span, limit_ref[0])
    last = cum[:, span - 1 :]
    flow = x_ref[...].astype(F32) * per_channel(step * jnp.exp(last - cum), table)
    high, low = split2(flow)
    b = b_ref[...]
    new_total = total[...] + last
    total[...] = new_total
    lane = iota((heads, TILE), 1)
    rows = per_channel(jnp.where(lane < 8, jnp.exp(last), jnp.exp(new_total)), table)
    new = state[...] * rows[0:1] + (dot(b, high, 0, 0) + dot(b, low, 0, 0))
    state[...] = new

    @pl.when(t == pl.num_programs(0) - 1)
    def _():
        wide = width // TILE
        steps, rows_dec, _ = dec_c_ref.shape
        for half in range(new.shape[0] // TILE):
            for col in range(wide):
                j = half * wide + col
                at = (pl.ds(half * TILE, TILE), pl.ds(col * TILE, TILE))
                out_ref[j, :TILE, :] = state[at]
                out_ref[j, TILE : TILE + 8, :] = rows[8:16, col * TILE : (col + 1) * TILE]
                for s in range(steps):
                    base = TILE + 8 + s * rows_dec
                    out_ref[j, base : base + rows_dec, :] = dec_c_ref[
                        s, :, half * TILE : (half + 1) * TILE
                    ].astype(F32)


def prefix_kernel(in_ref, out_ref):
    count = in_ref.shape[0]
    dec = in_ref.shape[1] - TILE - 8
    state = jnp.zeros((TILE, TILE), F32)
    for k in range(count):
        out_ref[k, :TILE, :] = state
        state = state * in_ref[k, TILE : TILE + 1, :] + in_ref[k, :TILE, :]
    high, low = split2(state)
    c = in_ref[:, TILE + 8 :, :].reshape(count * dec, TILE).astype(BF16)
    y = dot(c, high, 1, 0) + dot(c, low, 1, 0)
    out_ref[:, TILE:, :] = y.reshape(count, dec, TILE)


def local_kernel(
    limit_ref, rate_ref, skip_ref, dt_ref, x_ref, gate_ref, b_ref, c_ref,
    part_ref, coef_ref, state, total, skip,
):
    t = pl.program_id(0)
    heads, span = dt_ref.shape
    width = x_ref.shape[1]

    @pl.when(t == 0)
    def _():
        state[...] = jnp.zeros_like(state)
        total[...] = jnp.zeros_like(total)
        skip[...] = exact_dot(
            jnp.broadcast_to(skip_ref[...], (8, heads)), spread(heads, width)
        )

    table = spread3(heads, width)
    step, cum = head_terms(dt_ref, as_column(rate_ref[...]), t * span, limit_ref[0])
    last = cum[:, span - 1 :]
    b, c = b_ref[...], c_ref[...]
    x = x_ref[...].astype(F32)
    high, low = split2(x * per_channel(step * jnp.exp(-cum), table))
    lower = iota((span, span), 0) >= iota((span, span), 1)
    score_high, score_low = split2(jnp.where(lower, dot(c, b, 1, 1), 0.0))
    acc = dot(score_high, high, 1, 0) + dot(score_high, low, 1, 0) + dot(score_low, high, 1, 0)
    now = state[...]
    now_high, now_low = split2(now)
    acc = acc + dot(c, now_high, 1, 0) + dot(c, now_low, 1, 0)
    decay = per_channel(jnp.exp(cum), table)
    before = total[...]
    total[...] = before + last
    lane = iota((heads, TILE), 1)
    rows = per_channel(jnp.where(lane < 8, jnp.exp(last), jnp.exp(before)), table)
    live = t * span + iota((span, width), 0) < limit_ref[0]
    gate = jnp.where(live, silu(gate_ref[...].astype(F32)), 0.0)
    part_ref[...] = (acc * decay + skip[0:1] * x) * gate
    coef_ref[...] = decay * rows[8:9] * gate
    state[...] = (now + (dot(b, high, 0, 0) + dot(b, low, 0, 0))) * rows[0:1]


def decode_kernel(
    slots_ref, rate_ref, skip_ref, dt_ref, x_ref, gate_ref, b_ref, c_ref, state_ref,
    part_ref, coef_ref, x_all, gate_all, b_all, c_all, keep_log, size_all,
):
    d = pl.program_id(0)
    steps, seqs, width = x_ref.shape
    heads = dt_ref.shape[2]
    rows = steps * seqs

    @pl.when(d == 0)
    def _():
        total = jnp.zeros((seqs, heads), F32)
        for s in range(steps):
            at = pl.ds(s * seqs, seqs)
            size = jax.nn.softplus(dt_ref[s].astype(F32))
            total = total - size * rate_ref[...]
            keep_log[at, :] = total
            size_all[at, :] = size
            x_all[at, :] = x_ref[s].astype(F32)
            gate_all[at, :] = gate_ref[s].astype(F32)
            b_all[at, :] = b_ref[s].astype(F32)
            c_all[at, :] = c_ref[s].astype(F32)
        table = spread(heads, width)
        keep = exact_dot(jnp.exp(keep_log[...]), table)
        flow = exact_dot(size_all[...] * jnp.exp(-keep_log[...]), table) * x_all[...]
        scores = dot(c_all[...].astype(BF16), b_all[...].astype(BF16), 1, 1)
        row, col = iota((rows, rows), 0), iota((rows, rows), 1)
        same = (row % seqs == col % seqs) & (col <= row)
        inner = exact_dot(jnp.where(same, scores, 0.0), flow)
        skip = exact_dot(jnp.broadcast_to(skip_ref[...], (8, heads)), table)[0:1]
        gate = silu(gate_all[...])
        part_ref[...] = (keep * inner + skip * x_all[...]) * gate
        coef_ref[...] = keep * gate

    c = c_all[...].astype(BF16)
    high, low = split2(state_ref[0])
    own = dot(c, high, 1, 1) + dot(c, low, 1, 1)
    mine = iota((rows, 1), 0) % seqs == d
    take = mine & (slots_ref[d] < 0)
    part_ref[...] += jnp.where(take, own * coef_ref[...], 0.0)
    coef_ref[...] = jnp.where(take, 0.0, coef_ref[...])


def mix_kernel(
    in_ref, c_ref, part_ref, coef_ref, dec_part_ref, dec_coef_ref,
    mixed_ref, dec_mixed_ref, power_ref, high, low,
):
    t = pl.program_id(0)
    span = c_ref.shape[0]
    wide = part_ref.shape[1] // TILE

    @pl.when(t == 0)
    def _():
        power = jnp.zeros((dec_part_ref.shape[0], TILE), F32)
        for col in range(wide):
            cols = pl.ds(col * TILE, TILE)
            for half in range(in_ref.shape[0] // wide):
                at = (pl.ds(half * TILE, TILE), cols)
                high[at], low[at] = split2(in_ref[half * wide + col, :TILE, :])
            final = in_ref[col, TILE:, :] + in_ref[wide + col, TILE:, :]
            mixed = dec_part_ref[:, cols] + dec_coef_ref[:, cols] * final
            dec_mixed_ref[:, cols] = mixed
            power = power + mixed * mixed
        power_ref[...] = jnp.zeros_like(power_ref)
        power_ref[4:5, :] = as_row(jnp.sum(power, axis=1, keepdims=True), span)

    c = c_ref[...]
    mixed = part_ref[...] + coef_ref[...] * (dot(c, high[...], 1, 0) + dot(c, low[...], 1, 0))
    mixed_ref[...] = mixed
    power_ref[pl.ds(t, 1), :] = as_row(jnp.sum(mixed * mixed, axis=1, keepdims=True), span)


def norm_kernel(power_ref, other_ref, gain_ref, mixed_ref, dec_mixed_ref, out_ref, dec_ref, dec):
    t = pl.program_id(0)
    full = 2 * mixed_ref.shape[1]

    def scale(row):
        power = power_ref[pl.ds(row, 1), :] + other_ref[pl.ds(row, 1), :]
        return as_column(lax.rsqrt(power / full + EPS))

    out_ref[...] = (mixed_ref[...] * scale(t) * gain_ref[...]).astype(BF16)

    @pl.when(t == 0)
    def _():
        steps, seqs, _ = dec_ref.shape
        rows = steps * seqs
        dec[...] = dec_mixed_ref[...] * scale(4)[:rows] * gain_ref[...]
        for s in range(steps):
            dec_ref[s] = dec[s * seqs : (s + 1) * seqs, :].astype(BF16)


def params(mib):
    return pltpu.CompilerParams(
        dimension_semantics=("arbitrary",), vmem_limit_bytes=mib * 2**20
    )


def whole(shape):
    return pl.BlockSpec(shape, lambda t: (0,) * len(shape))


def by_rows(shape):
    return pl.BlockSpec(shape, lambda t: (t,) + (0,) * (len(shape) - 1))


def shards(
    x_in, gate_in, dt_raw, b_in, c_in, lengths, decay_rate, skip_gain, norm_gain,
    dec_states, dec_x, dec_gate, dec_dt, dec_b, dec_c, slots,
):
    _, length, _, width = x_in.shape
    heads, state = dt_raw.shape[3], b_in.shape[3]
    steps, seqs = dec_x.shape[:2]
    rows = steps * seqs
    count = lax.axis_size(SEQ)
    spans = length // SPAN
    limit = lengths - lax.axis_index(SEQ) * length
    x, gate = x_in.reshape(length, width), gate_in.reshape(length, width)
    dt = dt_raw.reshape(length, heads).T
    b, c = b_in.reshape(length, state), c_in.reshape(length, state)
    dec_x, dec_gate = dec_x.reshape(steps, seqs, width), dec_gate.reshape(steps, seqs, width)
    dec_b, dec_c = dec_b.reshape(steps, seqs, state), dec_c.reshape(steps, seqs, state)
    dec_dt = dec_dt.reshape(steps, seqs, heads)
    smem = pl.BlockSpec(memory_space=pltpu.SMEM)
    dt_spec = pl.BlockSpec((heads, SPAN), lambda t: (0, t))
    head_spec = whole((1, heads))
    wide_spec, state_spec = by_rows((SPAN, width)), by_rows((SPAN, state))
    sent_rows = TILE + 8 + rows
    back_rows = TILE + rows

    sent = pl.pallas_call(
        state_kernel,
        name="device_state",
        out_shape=jax.ShapeDtypeStruct((count, sent_rows, TILE), F32),
        grid=(spans,),
        in_specs=[smem, head_spec, dt_spec, wide_spec, state_spec, whole((steps, seqs, state))],
        out_specs=whole((count, sent_rows, TILE)),
        scratch_shapes=[pltpu.VMEM((state, width), F32), pltpu.VMEM((heads, TILE), F32)],
        compiler_params=params(24),
        cost_estimate=pl.CostEstimate(
            flops=8 * length * state * width, bytes_accessed=6 * 2**20, transcendentals=0
        ),
    )(limit, decay_rate, dt, x, b, dec_c)
    owned = lax.all_to_all(sent, SEQ, 0, 0)

    part, coef = pl.pallas_call(
        local_kernel,
        name="device_outputs",
        out_shape=[jax.ShapeDtypeStruct((length, width), F32)] * 2,
        grid=(spans,),
        in_specs=[
            smem, head_spec, head_spec, dt_spec, wide_spec, wide_spec, state_spec, state_spec,
        ],
        out_specs=[wide_spec, wide_spec],
        scratch_shapes=[
            pltpu.VMEM((state, width), F32),
            pltpu.VMEM((heads, TILE), F32),
            pltpu.VMEM((8, width), F32),
        ],
        compiler_params=params(32),
        cost_estimate=pl.CostEstimate(
            flops=20 * length * state * width, bytes_accessed=14 * 2**20, transcendentals=0
        ),
    )(limit, decay_rate, skip_gain, dt, x, gate, b, c)

    dec_part, dec_coef = pl.pallas_call(
        decode_kernel,
        name="decode_own",
        out_shape=[jax.ShapeDtypeStruct((rows, width), F32)] * 2,
        grid=(seqs,),
        in_specs=[
            smem, head_spec, head_spec, whole((steps, seqs, heads)),
            whole((steps, seqs, width)), whole((steps, seqs, width)),
            whole((steps, seqs, state)), whole((steps, seqs, state)),
            by_rows((1, width, state)),
        ],
        out_specs=[whole((rows, width))] * 2,
        scratch_shapes=[
            pltpu.VMEM((rows, width), F32), pltpu.VMEM((rows, width), F32),
            pltpu.VMEM((rows, state), F32), pltpu.VMEM((rows, state), F32),
            pltpu.VMEM((rows, heads), F32), pltpu.VMEM((rows, heads), F32),
        ],
        compiler_params=params(16),
        cost_estimate=pl.CostEstimate(
            flops=4 * seqs * 256 * state * width, bytes_accessed=5 * 2**20, transcendentals=0
        ),
    )(
        slots, decay_rate, skip_gain, dec_dt, dec_x, dec_gate, dec_b, dec_c,
        dec_states.reshape(seqs, width, state),
    )

    back = pl.pallas_call(
        prefix_kernel,
        name="prefix",
        out_shape=jax.ShapeDtypeStruct((count, back_rows, TILE), F32),
        compiler_params=pltpu.CompilerParams(vmem_limit_bytes=16 * 2**20),
        cost_estimate=pl.CostEstimate(
            flops=2 * count * rows * TILE * TILE, bytes_accessed=3 * 2**20, transcendentals=0
        ),
    )(owned)
    entry = lax.all_to_all(back, SEQ, 0, 0)

    mixed, dec_mixed, power = pl.pallas_call(
        mix_kernel,
        name="mix",
        out_shape=[
            jax.ShapeDtypeStruct((length, width), F32),
            jax.ShapeDtypeStruct((rows, width), F32),
            jax.ShapeDtypeStruct((8, SPAN), F32),
        ],
        grid=(spans,),
        in_specs=[
            whole((count, back_rows, TILE)), state_spec, wide_spec, wide_spec,
            whole((rows, width)), whole((rows, width)),
        ],
        out_specs=[wide_spec, whole((rows, width)), whole((8, SPAN))],
        scratch_shapes=[pltpu.VMEM((state, width), BF16), pltpu.VMEM((state, width), BF16)],
        compiler_params=params(24),
        cost_estimate=pl.CostEstimate(
            flops=4 * length * state * width, bytes_accessed=14 * 2**20, transcendentals=0
        ),
    )(entry, c, part, coef, dec_part, dec_coef)
    other = lax.ppermute(power, "pool", [(0, 1), (1, 0)])

    prefill_out, decode_out = pl.pallas_call(
        norm_kernel,
        name="norm",
        out_shape=[
            jax.ShapeDtypeStruct((length, width), BF16),
            jax.ShapeDtypeStruct((steps, seqs, width), BF16),
        ],
        grid=(spans,),
        in_specs=[
            whole((8, SPAN)), whole((8, SPAN)), whole((1, width)), wide_spec, whole((rows, width)),
        ],
        out_specs=[wide_spec, whole((steps, seqs, width))],
        scratch_shapes=[pltpu.VMEM((rows, width), F32)],
        compiler_params=params(16),
        cost_estimate=pl.CostEstimate(
            flops=4 * length * width, bytes_accessed=6 * 2**20, transcendentals=0
        ),
    )(power, other, norm_gain, mixed, dec_mixed)
    return (
        prefill_out.reshape(x_in.shape),
        decode_out.reshape(steps, seqs, 1, width),
    )


def solution(mesh):
    split = Mesh(
        mesh.devices.reshape(mesh.shape["pool"], 4, 4, mesh.shape["head"]),
        ("pool", "seq_0", "seq_1", "head"),
    )
    wide = P(None, SEQ, "head", "pool")
    shared = P(None, SEQ, "head", None)
    per_head = P("head", "pool")
    return jax.shard_map(
        shards,
        mesh=split,
        in_specs=(
            wide, wide, wide, shared, shared, P(), per_head, per_head, per_head,
            P(SEQ, "head", "pool", None, None), wide, wide, wide, shared, shared, P(SEQ),
        ),
        out_specs=(wide, wide),
        check_vma=False,
    )
```

profile of v0, /device:TPU:1, one launch (start us, length us, event | category | flops | bytes accessed | tf_op | source)
XLA Modules:
  0.0 74.6 jit_solution(16529605438359796161)
XLA Ops:
  1.3 0.0 copy-start.8
  1.3 0.7 copy-done.8
  2.0 0.0 copy-start.14
  2.0 0.7 copy-done.14
  2.7 0.0 copy-start.17
  2.7 1.6 %copy-done.17 = bf16[1,1024,1,1024]{3,1,2,0:T(8,128)(2,1)S(1)} copy-done((bf16[1,1024,1,1024]{3,1,2,0:T(8,128)(2,1)S(1)}, bf16[1,1024,1,1024]{3,1,2,0:T(8,128)(2,1)}, u32[]{:S(2)}) %copy-start.17) | copy-done | bytes 2097176
  4.2 0.0 copy-start.20
  4.3 1.0 %copy-done.20 = bf16[1,1024,1,256]{3,1,2,0:T(8,128)(2,1)S(1)} copy-done((bf16[1,1024,1,256]{3,1,2,0:T(8,128)(2,1)S(1)}, bf16[1,1024,1,256]{3,1,2,0:T(8,128)(2,1)}, u32[]{:S(2)}) %copy-start.20) | copy-done | bytes 524312
  5.3 0.0 copy-start.22
  5.3 0.8 %copy-done.22 = bf16[1,1024,1,16]{1,3,2,0:T(8,128)(2,1)S(1)} copy-done((bf16[1,1024,1,16]{1,3,2,0:T(8,128)(2,1)S(1)}, bf16[1,1024,1,16]{1,3,2,0:T(8,128)(2,1)}, u32[]{:S(2)}) %copy-start.22) | copy-done | bytes 32792
  6.1 4.3 %device_state.1 = f32[16,168,128]{2,1,0:T(8,128)S(1)} custom-call(s32[1]{0:T(128)S(6)} %sub.7.limit_ref, f32[1,16]{1,0:T(1,128)S(1)} %copy-done.14, bf16[16,1024]{1,0:T(8,128)(2,1)S(1)} %bitcast.32, bf16[1024,1024]{1,0:T(8,128)(2,1)S(1)} %bitcast.27, bf16[1024,256]{1,0:T(8,128)(2,1)S(1)} %bitcast.30, bf16[8,4,256]{2,1,0:T(4,128)(2,1)S(1)} %bitcast.23), custom_call_target="tpu_custom_call" | custom-call | flops 2147483648 | bytes 6291456 | tf_op jit(solution)/shard_map/device_state/pallas_call | solution.py:303
  10.4 26.7 %all_to_all.10.in_ref = f32[16,168,128]{2,1,0:T(8,128)S(1)} all-to-all(f32[16,168,128]{2,1,0:T(8,128)S(1)} %device_state.1), channel_id=1, replica_groups=mesh['pool'=2,'seq_0'=4,'seq_1'=4,'head'=8] {'seq_0','seq_1'}, dimensions={0} | all-to-all | bytes 2752512 | tf_op jit(solution)/shard_map/all_to_all | solution.py:316
  37.0 0.0 copy-start.7
  37.0 0.0 copy-start.11
  37.0 0.0 copy-start.13
  37.0 0.0 copy-start.15
  37.1 0.0 copy-start.16
  37.1 1.4 %prefix.1 = f32[16,160,128]{2,1,0:T(8,128)} custom-call(f32[16,168,128]{2,1,0:T(8,128)S(1)} %all_to_all.10.in_ref), custom_call_target="tpu_custom_call" | custom-call | flops 16777216 | bytes 3145728 | tf_op jit(solution)/shard_map/prefix/pallas_call | solution.py:364
  38.4 3.7 %all-to-all-start.1 = ((f32[16,160,128]{2,1,0:T(8,128)}), f32[16,160,128]{2,1,0:T(8,128)S(1)}, u32[]{:S(2)}, u32[]{:S(2)}) async-start(f32[16,160,128]{2,1,0:T(8,128)} %prefix.1), calls=%async_computation.1 | async-start | bytes 2621440 | tf_op jit(solution)/shard_map/all_to_all | solution.py:373
  42.2 0.0 copy-done.6
  42.2 0.0 copy-done.7
  42.2 0.0 copy-done.9
  42.2 0.0 copy-done.10
  42.2 0.0 copy-done.11
  42.2 0.0 copy-done.13
  42.2 0.0 copy-done.15
  42.2 0.0 copy-done.16
  42.3 0.0 copy-start
  42.3 2.2 %copy-done = f32[4,1,16,64,256]{4,3,2,1,0:T(8,128)S(1)} copy-done((f32[4,1,16,64,256]{4,3,2,1,0:T(8,128)S(1)}, f32[4,1,16,64,256]{4,3,2,1,0:T(8,128)}, u32[]{:S(2)}) %copy-start) | copy-done | bytes 4194328
  44.5 3.0 %decode_own.1 = (f32[32,1024]{1,0:T(8,128)S(1)}, f32[32,1024]{1,0:T(8,128)S(1)}) custom-call(s32[4]{0:T(128)S(1)} %copy-done.13, f32[1,16]{1,0:T(1,128)S(1)} %copy-done.15, f32[1,16]{1,0:T(1,128)S(1)} %copy-done.16, bf16[8,4,16]{2,1,0:T(4,128)(2,1)S(1)} %bitcast.26, bf16[8,4,1024]{2,1,0:T(4,128)(2,1)S(1)} %bitcast.21, bf16[8,4,1024]{2,1,0:T(4,128)(2,1)S(1)} %bitcast.22, ...), custom_call_target="tpu_custom_call" | custom-call | flops 1073741824 | bytes 5242880 | tf_op jit(solution)/shard_map/decode_own/pallas_call | solution.py:338
  47.4 0.0 copy-done.5
  47.4 0.0 copy-done.18
  47.5 0.0 copy-done.21
  47.5 0.0 copy-done.23
  47.5 0.0 copy-start.19
  47.5 1.6 %copy-done.19 = bf16[1,1024,1,1024]{3,1,2,0:T(8,128)(2,1)S(1)} copy-done((bf16[1,1024,1,1024]{3,1,2,0:T(8,128)(2,1)S(1)}, bf16[1,1024,1,1024]{3,1,2,0:T(8,128)(2,1)}, u32[]{:S(2)}) %copy-start.19) | copy-done | bytes 2097176
  49.1 9.3 %device_outputs.1 = (f32[1024,1024]{1,0:T(8,128)S(1)}, f32[1024,1024]{1,0:T(8,128)S(1)}) custom-call(s32[1]{0:T(128)S(6)} %sub.7.limit_ref, f32[1,16]{1,0:T(1,128)S(1)} %copy-done.15, f32[1,16]{1,0:T(1,128)S(1)} %copy-done.16, bf16[16,1024]{1,0:T(8,128)(2,1)S(1)} %bitcast.33, bf16[1024,1024]{1,0:T(8,128)(2,1)S(1)} %bitcast.28, ...), custom_call_target="tpu_custom_call" | custom-call | flops 5368709120 | bytes 14680064 | tf_op jit(solution)/shard_map/device_outputs/pallas_call | solution.py:318
  58.4 0.0 copy-start.1
  58.4 1.9 %copy-done.1 = f32[1024,1024]{1,0:T(8,128)} copy-done((f32[1024,1024]{1,0:T(8,128)}, f32[1024,1024]{1,0:T(8,128)S(1)}, u32[]{:S(2)}) %copy-start.1) | copy-done | bytes 4194328
  60.4 2.0 %copy-done.3 = f32[1024,1024]{1,0:T(8,128)} copy-done((f32[1024,1024]{1,0:T(8,128)}, f32[1024,1024]{1,0:T(8,128)S(1)}, u32[]{:S(2)}) %copy-start.3) | copy-done | bytes 4194328
  62.4 0.0 all-to-all-done.1.in_ref
  62.4 2.2 %copy-done.2 = f32[1024,1024]{1,0:T(8,128)S(1)} copy-done((f32[1024,1024]{1,0:T(8,128)S(1)}, f32[1024,1024]{1,0:T(8,128)}, u32[]{:S(2)}) %copy-start.2) | copy-done | bytes 4194328
  64.6 2.2 %copy-done.4 = f32[1024,1024]{1,0:T(8,128)S(1)} copy-done((f32[1024,1024]{1,0:T(8,128)S(1)}, f32[1024,1024]{1,0:T(8,128)}, u32[]{:S(2)}) %copy-start.4) | copy-done | bytes 4194328
  66.8 2.5 %mix.1 = (f32[1024,1024]{1,0:T(8,128)S(1)}, f32[32,1024]{1,0:T(8,128)S(1)}, f32[8,256]{1,0:T(8,128)S(1)}) custom-call(f32[16,160,128]{2,1,0:T(8,128)S(1)} %all-to-all-done.1.in_ref, bf16[1024,256]{1,0:T(8,128)(2,1)S(1)} %bitcast.20, f32[1024,1024]{1,0:T(8,128)S(1)} %copy-done.2, f32[1024,1024]{1,0:T(8,128)S(1)} %copy-done.4, ...), custom_call_target="tpu_custom_call" | custom-call | flops 1073741824 | bytes 14680064 | tf_op jit(solution)/shard_map/mix/pallas_call | solution.py:375
  69.3 2.2 %collective-permute-start = (f32[8,256]{1,0:T(8,128)S(1)}, f32[8,256]{1,0:T(8,128)S(1)}, u32[]{:S(2)}, u32[]{:S(2)}) collective-permute-start(f32[8,256]{1,0:T(8,128)S(1)} %get-tuple-element.15.power_ref), channel_id=1, source_target_pairs={{0,128},{128,0},{1,129},{129,1},{2,130},{130,2},{3,131},{131,3},{4... | collective-permute-start | bytes 24584 | tf_op jit(solution)/shard_map/ppermute | solution.py:395
  71.5 0.8 %collective-permute-done.other_ref = f32[8,256]{1,0:T(8,128)S(1)} collective-permute-done((f32[8,256]{1,0:T(8,128)S(1)}, f32[8,256]{1,0:T(8,128)S(1)}, u32[]{:S(2)}, u32[]{:S(2)}) %collective-permute-start) | collective-permute-done | bytes 8224 | tf_op jit(solution)/shard_map/ppermute | solution.py:395
  72.3 0.0 copy-done.12
  72.3 2.3 %norm.1 = (bf16[1024,1024]{1,0:T(8,128)(2,1)}, bf16[8,4,1024]{2,1,0:T(4,128)(2,1)}) custom-call(f32[8,256]{1,0:T(8,128)S(1)} %get-tuple-element.15.power_ref, f32[8,256]{1,0:T(8,128)S(1)} %collective-permute-done.other_ref, f32[1,1024]{1,0:T(1,128)S(1)} %copy-done.12, f32[1024,1024]{1,0:T(8,128)S(1)} %get-tuple-element.16.mixed_ref, ...), custom_call_target="tpu_custom_call" | custom-call | flops 4194304 | bytes 6291456 | tf_op jit(solution)/shard_map/norm/pallas_call | solution.py:397
  (11 shorter events, 0.0 us)
Async XLA Ops:
  1.3 0.7 copy-start.8
  2.0 0.7 copy-start.14
  2.7 1.6 %copy-start.17 = (bf16[1,1024,1,1024]{3,1,2,0:T(8,128)(2,1)S(1)}, bf16[1,1024,1,1024]{3,1,2,0:T(8,128)(2,1)}, u32[]{:S(2)}) copy-start(bf16[1,1024,1,1024]{3,1,2,0:T(8,128)(2,1)} %param.16) | copy-start | bytes 6291460
  4.2 1.0 %copy-start.20 = (bf16[1,1024,1,256]{3,1,2,0:T(8,128)(2,1)S(1)}, bf16[1,1024,1,256]{3,1,2,0:T(8,128)(2,1)}, u32[]{:S(2)}) copy-start(bf16[1,1024,1,256]{3,1,2,0:T(8,128)(2,1)} %param.19) | copy-start | bytes 1572868
  5.3 0.8 %copy-start.22 = (bf16[1,1024,1,16]{1,3,2,0:T(8,128)(2,1)S(1)}, bf16[1,1024,1,16]{1,3,2,0:T(8,128)(2,1)}, u32[]{:S(2)}) copy-start(bf16[1,1024,1,16]{1,3,2,0:T(8,128)(2,1)} %param.18) | copy-start | bytes 98308
  37.0 5.2 %copy-start.6 = (bf16[8,4,1,1024]{3,1,2,0:T(4,128)(2,1)S(1)}, bf16[8,4,1,1024]{3,1,2,0:T(4,128)(2,1)}, u32[]{:S(2)}) copy-start(bf16[8,4,1,1024]{3,1,2,0:T(4,128)(2,1)} %param.26) | copy-start | bytes 196612
  37.0 5.2 %copy-start.7 = (bf16[8,4,1,1024]{3,1,2,0:T(4,128)(2,1)S(1)}, bf16[8,4,1,1024]{3,1,2,0:T(4,128)(2,1)}, u32[]{:S(2)}) copy-start(bf16[8,4,1,1024]{3,1,2,0:T(4,128)(2,1)} %param.27) | copy-start | bytes 196612
  37.0 5.2 %copy-start.9 = (bf16[8,4,1,256]{3,1,2,0:T(4,128)(2,1)S(1)}, bf16[8,4,1,256]{3,1,2,0:T(4,128)(2,1)}, u32[]{:S(2)}) copy-start(bf16[8,4,1,256]{3,1,2,0:T(4,128)(2,1)} %param.30) | copy-start | bytes 49156
  37.0 5.2 %copy-start.10 = (bf16[8,4,1,256]{3,1,2,0:T(4,128)(2,1)S(1)}, bf16[8,4,1,256]{3,1,2,0:T(4,128)(2,1)}, u32[]{:S(2)}) copy-start(bf16[8,4,1,256]{3,1,2,0:T(4,128)(2,1)} %param.29) | copy-start | bytes 49156
  37.0 5.2 %copy-start.11 = (bf16[8,4,1,16]{3,1,2,0:T(4,128)(2,1)S(1)}, bf16[8,4,1,16]{3,1,2,0:T(4,128)(2,1)}, u32[]{:S(2)}) copy-start(bf16[8,4,1,16]{3,1,2,0:T(4,128)(2,1)} %param.28) | copy-start | bytes 3076
  37.0 5.2 %copy-start.13 = (s32[4]{0:T(128)S(1)}, s32[4]{0:T(128)}, u32[]{:S(2)}) copy-start(s32[4]{0:T(128)} %slots_ref.1) | copy-start | bytes 52
  37.0 5.2 %copy-start.15 = (f32[1,16]{1,0:T(1,128)S(1)}, f32[1,16]{1,0:T(1,128)}, u32[]{:S(2)}) copy-start(f32[1,16]{1,0:T(1,128)} %rate_ref.5) | copy-start | bytes 196
  37.1 5.2 %copy-start.16 = (f32[1,16]{1,0:T(1,128)S(1)}, f32[1,16]{1,0:T(1,128)}, u32[]{:S(2)}) copy-start(f32[1,16]{1,0:T(1,128)} %skip_ref.3) | copy-start | bytes 196
  38.4 24.0 %all-to-all-start.1 = ((f32[16,160,128]{2,1,0:T(8,128)}), f32[16,160,128]{2,1,0:T(8,128)S(1)}, u32[]{:S(2)}, u32[]{:S(2)}) async-start(f32[16,160,128]{2,1,0:T(8,128)} %prefix.1), calls=%async_computation.1 | async-start | bytes 2621440 | tf_op jit(solution)/shard_map/all_to_all | solution.py:373
  42.3 2.2 %copy-start = (f32[4,1,16,64,256]{4,3,2,1,0:T(8,128)S(1)}, f32[4,1,16,64,256]{4,3,2,1,0:T(8,128)}, u32[]{:S(2)}) copy-start(f32[4,1,16,64,256]{4,3,2,1,0:T(8,128)} %param.25) | copy-start | bytes 12582916
  44.4 3.0 %copy-start.5 = (bf16[1,1024,1,256]{3,1,2,0:T(8,128)(2,1)S(1)}, bf16[1,1024,1,256]{3,1,2,0:T(8,128)(2,1)}, u32[]{:S(2)}) copy-start(bf16[1,1024,1,256]{3,1,2,0:T(8,128)(2,1)} %param.20) | copy-start | bytes 1572868
  44.4 3.0 %copy-start.18 = (bf16[1,1024,1,1024]{3,1,2,0:T(8,128)(2,1)S(1)}, bf16[1,1024,1,1024]{3,1,2,0:T(8,128)(2,1)}, u32[]{:S(2)}) copy-start(bf16[1,1024,1,1024]{3,1,2,0:T(8,128)(2,1)} %param.16) | copy-start | bytes 6291460
  44.5 3.0 %copy-start.21 = (bf16[1,1024,1,256]{3,1,2,0:T(8,128)(2,1)S(1)}, bf16[1,1024,1,256]{3,1,2,0:T(8,128)(2,1)}, u32[]{:S(2)}) copy-start(bf16[1,1024,1,256]{3,1,2,0:T(8,128)(2,1)} %param.19) | copy-start | bytes 1572868
  44.5 3.0 %copy-start.23 = (bf16[1,1024,1,16]{1,3,2,0:T(8,128)(2,1)S(1)}, bf16[1,1024,1,16]{1,3,2,0:T(8,128)(2,1)}, u32[]{:S(2)}) copy-start(bf16[1,1024,1,16]{1,3,2,0:T(8,128)(2,1)} %param.18) | copy-start | bytes 98308
  47.5 1.6 %copy-start.19 = (bf16[1,1024,1,1024]{3,1,2,0:T(8,128)(2,1)S(1)}, bf16[1,1024,1,1024]{3,1,2,0:T(8,128)(2,1)}, u32[]{:S(2)}) copy-start(bf16[1,1024,1,1024]{3,1,2,0:T(8,128)(2,1)} %param.17) | copy-start | bytes 6291460
  58.4 2.0 %copy-start.1 = (f32[1024,1024]{1,0:T(8,128)}, f32[1024,1024]{1,0:T(8,128)S(1)}, u32[]{:S(2)}) copy-start(f32[1024,1024]{1,0:T(8,128)S(1)} %get-tuple-element.11.part_ref) | copy-start | bytes 12582916
  60.4 2.0 %copy-start.3 = (f32[1024,1024]{1,0:T(8,128)}, f32[1024,1024]{1,0:T(8,128)S(1)}, u32[]{:S(2)}) copy-start(f32[1024,1024]{1,0:T(8,128)S(1)} %get-tuple-element.12.coef_ref) | copy-start | bytes 12582916
  62.4 2.2 %copy-start.2 = (f32[1024,1024]{1,0:T(8,128)S(1)}, f32[1024,1024]{1,0:T(8,128)}, u32[]{:S(2)}) copy-start(f32[1024,1024]{1,0:T(8,128)} %copy-done.1) | copy-start | bytes 12582916
  64.6 2.2 %copy-start.4 = (f32[1024,1024]{1,0:T(8,128)S(1)}, f32[1024,1024]{1,0:T(8,128)}, u32[]{:S(2)}) copy-start(f32[1024,1024]{1,0:T(8,128)} %copy-done.3) | copy-start | bytes 12582916
  66.8 5.6 %copy-start.12 = (f32[1,1024]{1,0:T(1,128)S(1)}, f32[1,1024]{1,0:T(1,128)}, u32[]{:S(2)}) copy-start(f32[1,1024]{1,0:T(1,128)} %gain_ref.1) | copy-start | bytes 12292
  69.3 3.1 %collective-permute-start = (f32[8,256]{1,0:T(8,128)S(1)}, f32[8,256]{1,0:T(8,128)S(1)}, u32[]{:S(2)}, u32[]{:S(2)}) collective-permute-start(f32[8,256]{1,0:T(8,128)S(1)} %get-tuple-element.15.power_ref), channel_id=1, source_target_pairs={{0,128},{128,0},{1,129},{129,1},{2,130},{130,2},{3,131},{131,3},{4... | collective-permute-start | bytes 24584 | tf_op jit(solution)/shard_map/ppermute | solution.py:395
where the time goes:
time: 75.2 us; the launch traced here: 74.6 us
  blocking collectives  26.7 us (36%)
  Pallas kernels  22.7 us (30%)
  local copies, waits for them, and re-layouts  16.9 us (22%)
  starting transfers between devices  5.97 us (8%)
  between operations  1.5 us (2%)
  waiting for transfers between devices  0.83 us (1%)
    all_to_all x1, blocking collectives, shards(): owned = lax.all_to_all(sent, SEQ, 0, 0)  26.7 us
    unnamed x48, local copies, waits for them, and re-layouts  16.9 us
    pallas_call x1, Pallas kernels, shards(): pl.pallas_call(local_kernel, name='device_outputs', out_shape=[jax.ShapeD...  9.33 us
    pallas_call x1, Pallas kernels, shards(): pl.pallas_call(state_kernel, name='device_state', out_shape=jax.ShapeDtyp...  4.29 us
    all_to_all x1, starting transfers between devices, shards(): entry = lax.all_to_all(back, SEQ, 0, 0)  3.74 us
    pallas_call x1, Pallas kernels, shards(): pl.pallas_call(decode_kernel, name='decode_own', out_shape=[jax.ShapeDtyp...  2.97 us
    pallas_call x1, Pallas kernels, shards(): pl.pallas_call(mix_kernel, name='mix', out_shape=[jax.ShapeDtypeStruct((l...  2.5 us
    pallas_call x1, Pallas kernels, shards(): pl.pallas_call(norm_kernel, name='norm', out_shape=[jax.ShapeDtypeStruct(...  2.27 us
  transfers between devices with their start and end apart: 2, of which 1 were waited for; matrix products, arithmetic and copies ran while one was open for 0% of the time, Pallas kernels for 16%

commit v1 on v0

--- a/solution.py
+++ b/solution.py
@@ -78,7 +78,7 @@
     return step, sums[:heads] + sums[heads : 2 * heads] + sums[2 * heads :]
 
 
-def state_kernel(limit_ref, rate_ref, dt_ref, x_ref, b_ref, dec_c_ref, out_ref, state, total):
+def state_kernel(lengths_ref, rate_ref, dt_ref, x_ref, b_ref, dec_c_ref, out_ref, state, total):
     t = pl.program_id(0)
     heads, span = dt_ref.shape
     width = x_ref.shape[1]
@@ -89,7 +89,8 @@
         total[...] = jnp.zeros_like(total)
 
     table = spread3(heads, width)
-    step, cum = head_terms(dt_ref, as_column(rate_ref[...]), t * span, limit_ref[0])
+    limit = lengths_ref[0] - lax.axis_index(SEQ) * (pl.num_programs(0) * span)
+    step, cum = head_terms(dt_ref, as_column(rate_ref[...]), t * span, limit)
     last = cum[:, span - 1 :]
     flow = x_ref[...].astype(F32) * per_channel(step * jnp.exp(last - cum), table)
     high, low = split2(flow)
@@ -132,8 +133,8 @@
 
 
 def local_kernel(
-    limit_ref, rate_ref, skip_ref, dt_ref, x_ref, gate_ref, b_ref, c_ref,
-    part_ref, coef_ref, state, total, skip,
+    lengths_ref, rate_ref, skip_ref, dt_ref, x_ref, gate_ref, b_ref, c_ref,
+    part_ref, state, total, skip,
 ):
     t = pl.program_id(0)
     heads, span = dt_ref.shape
@@ -148,7 +149,8 @@
         )
 
     table = spread3(heads, width)
-    step, cum = head_terms(dt_ref, as_column(rate_ref[...]), t * span, limit_ref[0])
+    limit = lengths_ref[0] - lax.axis_index(SEQ) * (pl.num_programs(0) * span)
+    step, cum = head_terms(dt_ref, as_column(rate_ref[...]), t * span, limit)
     last = cum[:, span - 1 :]
     b, c = b_ref[...], c_ref[...]
     x = x_ref[...].astype(F32)
@@ -164,10 +166,10 @@
     total[...] = before + last
     lane = iota((heads, TILE), 1)
     rows = per_channel(jnp.where(lane < 8, jnp.exp(last), jnp.exp(before)), table)
-    live = t * span + iota((span, width), 0) < limit_ref[0]
+    live = t * span + iota((span, width), 0) < limit
     gate = jnp.where(live, silu(gate_ref[...].astype(F32)), 0.0)
-    part_ref[...] = (acc * decay + skip[0:1] * x) * gate
-    coef_ref[...] = decay * rows[8:9] * gate
+    part_ref[0] = (acc * decay + skip[0:1] * x) * gate
+    part_ref[1] = decay * rows[8:9] * gate
     state[...] = (now + (dot(b, high, 0, 0) + dot(b, low, 0, 0))) * rows[0:1]
 
 
@@ -215,12 +217,12 @@
 
 
 def mix_kernel(
-    in_ref, c_ref, part_ref, coef_ref, dec_part_ref, dec_coef_ref,
+    in_ref, c_ref, part_ref, dec_part_ref, dec_coef_ref,
     mixed_ref, dec_mixed_ref, power_ref, high, low,
 ):
     t = pl.program_id(0)
     span = c_ref.shape[0]
-    wide = part_ref.shape[1] // TILE
+    wide = part_ref.shape[2] // TILE
 
     @pl.when(t == 0)
     def _():
@@ -238,7 +240,7 @@
         power_ref[4:5, :] = as_row(jnp.sum(power, axis=1, keepdims=True), span)
 
     c = c_ref[...]
-    mixed = part_ref[...] + coef_ref[...] * (dot(c, high[...], 1, 0) + dot(c, low[...], 1, 0))
+    mixed = part_ref[0] + part_ref[1] * (dot(c, high[...], 1, 0) + dot(c, low[...], 1, 0))
     mixed_ref[...] = mixed
     power_ref[pl.ds(t, 1), :] = as_row(jnp.sum(mixed * mixed, axis=1, keepdims=True), span)
 
@@ -274,6 +276,14 @@
 
 def by_rows(shape):
     return pl.BlockSpec(shape, lambda t: (t,) + (0,) * (len(shape) - 1))
+
+
+def in_hbm(v):
+    return pltpu.with_memory_space_constraint(v, pltpu.HBM)
+
+
+def in_vmem(v):
+    return pltpu.with_memory_space_constraint(v, pltpu.VMEM)
 
 
 def shards(
@@ -286,7 +296,6 @@
     rows = steps * seqs
     count = lax.axis_size(SEQ)
     spans = length // SPAN
-    limit = lengths - lax.axis_index(SEQ) * length
     x, gate = x_in.reshape(length, width), gate_in.reshape(length, width)
     dt = dt_raw.reshape(length, heads).T
     b, c = b_in.reshape(length, state), c_in.reshape(length, state)
@@ -296,6 +305,7 @@
     smem = pl.BlockSpec(memory_space=pltpu.SMEM)
     dt_spec = pl.BlockSpec((heads, SPAN), lambda t: (0, t))
     head_spec = whole((1, heads))
+    pair_spec = pl.BlockSpec((2, SPAN, width), lambda t: (0, t, 0))
     wide_spec, state_spec = by_rows((SPAN, width)), by_rows((SPAN, state))
     sent_rows = TILE + 8 + rows
     back_rows = TILE + rows
@@ -312,18 +322,18 @@
         cost_estimate=pl.CostEstimate(
             flops=8 * length * state * width, bytes_accessed=6 * 2**20, transcendentals=0
         ),
-    )(limit, decay_rate, dt, x, b, dec_c)
+    )(lengths, *map(in_hbm, (decay_rate, dt, x, b, dec_c)))
     owned = lax.all_to_all(sent, SEQ, 0, 0)
 
-    part, coef = pl.pallas_call(
+    parts = pl.pallas_call(
         local_kernel,
         name="device_outputs",
-        out_shape=[jax.ShapeDtypeStruct((length, width), F32)] * 2,
+        out_shape=pltpu.HBM((2, length, width), F32),
         grid=(spans,),
         in_specs=[
             smem, head_spec, head_spec, dt_spec, wide_spec, wide_spec, state_spec, state_spec,
         ],
-        out_specs=[wide_spec, wide_spec],
+        out_specs=pair_spec,
         scratch_shapes=[
             pltpu.VMEM((state, width), F32),
             pltpu.VMEM((heads, TILE), F32),
@@ -333,7 +343,7 @@
         cost_estimate=pl.CostEstimate(
             flops=20 * length * state * width, bytes_accessed=14 * 2**20, transcendentals=0
         ),
-    )(limit, decay_rate, skip_gain, dt, x, gate, b, c)
+    )(lengths, *map(in_hbm, (decay_rate, skip_gain, dt, x, gate, b, c)))
 
     dec_part, dec_coef = pl.pallas_call(
         decode_kernel,
@@ -357,10 +367,14 @@
             flops=4 * seqs * 256 * state * width, bytes_accessed=5 * 2**20, transcendentals=0
         ),
     )(
-        slots, decay_rate, skip_gain, dec_dt, dec_x, dec_gate, dec_b, dec_c,
-        dec_states.reshape(seqs, width, state),
-    )
-
+        slots,
+        *map(in_hbm, (decay_rate, skip_gain, dec_dt, dec_x, dec_gate, dec_b, dec_c)),
+        in_hbm(dec_states.reshape(seqs, width, state)),
+    )
+
+    owned, parts, dec_part, dec_coef = lax.optimization_barrier(
+        (owned, parts, dec_part, dec_coef)
+    )
     back = pl.pallas_call(
         prefix_kernel,
         name="prefix",
@@ -376,22 +390,22 @@
         mix_kernel,
         name="mix",
         out_shape=[
-            jax.ShapeDtypeStruct((length, width), F32),
+            pltpu.VMEM((length, width), F32),
             jax.ShapeDtypeStruct((rows, width), F32),
             jax.ShapeDtypeStruct((8, SPAN), F32),
         ],
         grid=(spans,),
         in_specs=[
-            whole((count, back_rows, TILE)), state_spec, wide_spec, wide_spec,
+            whole((count, back_rows, TILE)), state_spec, pair_spec,
             whole((rows, width)), whole((rows, width)),
         ],
         out_specs=[wide_spec, whole((rows, width)), whole((8, SPAN))],
         scratch_shapes=[pltpu.VMEM((state, width), BF16), pltpu.VMEM((state, width), BF16)],
-        compiler_params=params(24),
+        compiler_params=params(40),
         cost_estimate=pl.CostEstimate(
             flops=4 * length * state * width, bytes_accessed=14 * 2**20, transcendentals=0
         ),
-    )(entry, c, part, coef, dec_part, dec_coef)
+    )(entry, c, parts, dec_part, dec_coef)
     other = lax.ppermute(power, "pool", [(0, 1), (1, 0)])
 
     prefill_out, decode_out = pl.pallas_call(

time: 75.2 us -> 68.7 us (0.914)
  local copies, waits for them, and re-layouts: 16.9 us -> 0.01 us
  Pallas kernels: 22.7 us -> 31 us
  starting transfers between devices: 5.97 us -> 11.9 us
  blocking collectives: 26.7 us -> 21.1 us
  waiting for transfers between devices: 0.83 us -> 2.99 us
    unnamed x48 -> x6, local copies, waits for them, and re-layouts: 16.9 us -> 0.01 us
    all_to_all x1, blocking collectives: 26.7 us -> 21.1 us  [shards(): entry = lax.all_to_all(back, SEQ, 0, 0)]
    pallas_call x2, Pallas kernels: 11.8 us -> 17.3 us  [the longest x1 11.9 us: shards(): pl.pallas_call(local_kernel, name='device_outputs', out_shape=pltpu.HBM((...]
    all_to_all x1, starting transfers between devices: 3.74 us -> 7.72 us  [shards(): owned = lax.all_to_all(sent, SEQ, 0, 0)]
    pallas_call x1, Pallas kernels: 4.29 us -> 6.49 us  [shards(): pl.pallas_call(state_kernel, name='device_state', out_shape=jax.ShapeDtyp...]
    all_to_all x1, waiting for transfers between devices: 0.01 us -> 2.17 us  [shards(): owned = lax.all_to_all(sent, SEQ, 0, 0)]
    ppermute x1, starting transfers between devices: 2.23 us -> 4.2 us  [shards(): other = lax.ppermute(power, 'pool', [(0, 1), (1, 0)])]
    pallas_call x1, Pallas kernels: 2.97 us -> 4.6 us  [shards(): pl.pallas_call(decode_kernel, name='decode_own', out_shape=[jax.ShapeDtyp...]
  transfers between devices with their start and end apart: 2 -> 2, of which waited for: 1 -> 2; matrix products, arithmetic and copies ran while one was open for 0% -> 0% of each run, Pallas kernels for 16% -> 24%
where the time goes in v1:
time: 68.7 us; the launch traced here: 68.3 us
  Pallas kernels  31 us (45%)
  blocking collectives  21.1 us (31%)
  starting transfers between devices  11.9 us (17%)
  waiting for transfers between devices  2.99 us (4%)
  between operations  1.32 us (2%)
    all_to_all x1, blocking collectives, shards(): entry = lax.all_to_all(back, SEQ, 0, 0)  21.1 us
    pallas_call x1, Pallas kernels, shards(): pl.pallas_call(local_kernel, name='device_outputs', out_shape=pltpu.HBM((...  11.9 us
    all_to_all x1, starting transfers between devices, shards(): owned = lax.all_to_all(sent, SEQ, 0, 0)  7.72 us
    pallas_call x1, Pallas kernels, shards(): pl.pallas_call(state_kernel, name='device_state', out_shape=jax.ShapeDtyp...  6.49 us
    pallas_call x1, Pallas kernels, shards(): pl.pallas_call(mix_kernel, name='mix', out_shape=[pltpu.VMEM((length, wid...  5.39 us
    pallas_call x1, Pallas kernels, shards(): pl.pallas_call(decode_kernel, name='decode_own', out_shape=[jax.ShapeDtyp...  4.6 us
    ppermute x1, starting transfers between devices, shards(): other = lax.ppermute(power, 'pool', [(0, 1), (1, 0)])  4.2 us
    pallas_call x1, Pallas kernels, shards(): pl.pallas_call(norm_kernel, name='norm', out_shape=[jax.ShapeDtypeStruct(...  2.27 us
  transfers between devices with their start and end apart: 2, of which 2 were waited for; matrix products, arithmetic and copies ran while one was open for 0% of the time, Pallas kernels for 24%

profile of v1, /device:TPU:1, one launch (start us, length us, event | category | flops | bytes accessed | tf_op | source)
XLA Modules:
  0.0 68.3 jit_solution(11407658038175485288)
XLA Ops:
  1.3 6.5 %device_state.1 = f32[16,168,128]{2,1,0:T(8,128)} custom-call(s32[1]{0:T(128)S(6)} %copy.19.lengths_ref, f32[1,16]{1,0:T(1,128)} %rate_ref.5, bf16[16,1024]{1,0:T(8,128)(2,1)} %bitcast.33, bf16[1024,1024]{1,0:T(8,128)(2,1)} %bitcast.26, bf16[1024,256]{1,0:T(8,128)(2,1)} %bitcast.30, bf16[8,4,256]{2,1,0:T(4,128)(2,1)} %bitcast.22), custom_call_target="tpu_custom_call" | custom-call | flops 2147483648 | bytes 6291456 | tf_op jit(solution)/shard_map/device_state/pallas_call | solution.py:313
  7.8 0.0 copy-start.2
  7.8 7.7 %all-to-all-start = ((f32[16,168,128]{2,1,0:T(8,128)}), f32[16,168,128]{2,1,0:T(8,128)S(1)}, u32[]{:S(2)}, u32[]{:S(2)}) async-start(f32[16,168,128]{2,1,0:T(8,128)} %device_state.1), calls=%async_computation | async-start | bytes 2752512 | tf_op jit(solution)/shard_map/all_to_all | solution.py:326
  15.5 0.0 copy-done.2
  15.5 4.6 %decode_own.1 = (f32[32,1024]{1,0:T(8,128)S(1)}, f32[32,1024]{1,0:T(8,128)S(1)}) custom-call(s32[4]{0:T(128)S(1)} %copy-done.2, f32[1,16]{1,0:T(1,128)} %rate_ref.5, f32[1,16]{1,0:T(1,128)} %skip_ref.3, bf16[8,4,16]{2,1,0:T(4,128)(2,1)} %bitcast.25, bf16[8,4,1024]{2,1,0:T(4,128)(2,1)} %bitcast.20, bf16[8,4,1024]{2,1,0:T(4,128)(2,1)} %bitcast.21, ...), custom_call_target="tpu_custom_call" | custom-call | flops 1073741824 | bytes 5242880 | tf_op jit(solution)/shard_map/decode_own/pallas_call | solution.py:348
  20.1 11.9 %device_outputs.1.part_ref = f32[2,1024,1024]{2,1,0:T(8,128)} custom-call(s32[1]{0:T(128)S(6)} %copy.19.lengths_ref, f32[1,16]{1,0:T(1,128)} %rate_ref.5, f32[1,16]{1,0:T(1,128)} %skip_ref.3, bf16[16,1024]{1,0:T(8,128)(2,1)} %bitcast.34, bf16[1024,1024]{1,0:T(8,128)(2,1)} %bitcast.27, bf16[1024,1024]{1,0:T(8,128)(2,1)} %bitcast.28, ...), custom_call_target="tpu_custom_call" | custom-call | flops 5368709120 | bytes 14680064 | tf_op jit(solution)/shard_map/device_outputs/pallas_call | solution.py:328
  32.0 2.2 %all-to-all-done.in_ref = f32[16,168,128]{2,1,0:T(8,128)S(1)} async-done(((f32[16,168,128]{2,1,0:T(8,128)}), f32[16,168,128]{2,1,0:T(8,128)S(1)}, u32[]{:S(2)}, u32[]{:S(2)}) %all-to-all-start) | async-done | bytes 1376288 | tf_op jit(solution)/shard_map/all_to_all | solution.py:326
  34.2 0.0 copy-start
  34.2 0.3 prefix.1
  34.5 21.1 %all_to_all.10.in_ref = f32[16,160,128]{2,1,0:T(8,128)S(1)} all-to-all(f32[16,160,128]{2,1,0:T(8,128)S(1)} %prefix.1), channel_id=1, replica_groups=mesh['pool'=2,'seq_0'=4,'seq_1'=4,'head'=8] {'seq_0','seq_1'}, dimensions={0} | all-to-all | bytes 2621440 | tf_op jit(solution)/shard_map/all_to_all | solution.py:387
  55.6 0.0 copy-done
  55.6 0.0 copy-start.1
  55.6 5.4 %mix.1 = (f32[1024,1024]{1,0:T(8,128)S(1)}, f32[32,1024]{1,0:T(8,128)S(1)}, f32[8,256]{1,0:T(8,128)S(1)}) custom-call(f32[16,160,128]{2,1,0:T(8,128)S(1)} %all_to_all.10.in_ref, bf16[1024,256]{1,0:T(8,128)(2,1)S(1)} %bitcast.18, f32[2,1024,1024]{2,1,0:T(8,128)} %device_outputs.1.part_ref, f32[32,1024]{1,0:T(8,128)S(1)} %get-tuple-element.17.dec_part_ref, ...), custom_call_target="tpu_custom_call" | custom-call | flops 1073741824 | bytes 14680064 | tf_op jit(solution)/shard_map/mix/pallas_call | solution.py:389
  61.0 4.2 %collective-permute-start = (f32[8,256]{1,0:T(8,128)S(1)}, f32[8,256]{1,0:T(8,128)S(1)}, u32[]{:S(2)}, u32[]{:S(2)}) collective-permute-start(f32[8,256]{1,0:T(8,128)S(1)} %get-tuple-element.19.power_ref), channel_id=1, source_target_pairs={{0,128},{128,0},{1,129},{129,1},{2,130},{130,2},{3,131},{131,3},{4... | collective-permute-start | bytes 24584 | tf_op jit(solution)/shard_map/ppermute | solution.py:409
  65.2 0.8 %collective-permute-done.other_ref = f32[8,256]{1,0:T(8,128)S(1)} collective-permute-done((f32[8,256]{1,0:T(8,128)S(1)}, f32[8,256]{1,0:T(8,128)S(1)}, u32[]{:S(2)}, u32[]{:S(2)}) %collective-permute-start) | collective-permute-done | bytes 8224 | tf_op jit(solution)/shard_map/ppermute | solution.py:409
  66.0 0.0 copy-done.1
  66.0 2.3 %norm.1 = (bf16[1024,1024]{1,0:T(8,128)(2,1)}, bf16[8,4,1024]{2,1,0:T(4,128)(2,1)}) custom-call(f32[8,256]{1,0:T(8,128)S(1)} %get-tuple-element.19.power_ref, f32[8,256]{1,0:T(8,128)S(1)} %collective-permute-done.other_ref, f32[1,1024]{1,0:T(1,128)S(1)} %copy-done.1, f32[1024,1024]{1,0:T(8,128)S(1)} %get-tuple-element.20.mixed_ref, ...), custom_call_target="tpu_custom_call" | custom-call | flops 4194304 | bytes 6291456 | tf_op jit(solution)/shard_map/norm/pallas_call | solution.py:411
Async XLA Ops:
  7.8 7.7 %copy-start.2 = (s32[4]{0:T(128)S(1)}, s32[4]{0:T(128)}, u32[]{:S(2)}) copy-start(s32[4]{0:T(128)} %slots_ref.1) | copy-start | bytes 52
  7.8 26.4 %all-to-all-start = ((f32[16,168,128]{2,1,0:T(8,128)}), f32[16,168,128]{2,1,0:T(8,128)S(1)}, u32[]{:S(2)}, u32[]{:S(2)}) async-start(f32[16,168,128]{2,1,0:T(8,128)} %device_state.1), calls=%async_computation | async-start | bytes 2752512 | tf_op jit(solution)/shard_map/all_to_all | solution.py:326
  34.2 21.4 %copy-start = (bf16[1,1024,1,256]{3,1,2,0:T(8,128)(2,1)S(1)}, bf16[1,1024,1,256]{3,1,2,0:T(8,128)(2,1)}, u32[]{:S(2)}) copy-start(bf16[1,1024,1,256]{3,1,2,0:T(8,128)(2,1)} %param.20) | copy-start | bytes 1572868
  55.6 10.4 %copy-start.1 = (f32[1,1024]{1,0:T(1,128)S(1)}, f32[1,1024]{1,0:T(1,128)}, u32[]{:S(2)}) copy-start(f32[1,1024]{1,0:T(1,128)} %gain_ref.1) | copy-start | bytes 12292
  61.0 5.0 %collective-permute-start = (f32[8,256]{1,0:T(8,128)S(1)}, f32[8,256]{1,0:T(8,128)S(1)}, u32[]{:S(2)}, u32[]{:S(2)}) collective-permute-start(f32[8,256]{1,0:T(8,128)S(1)} %get-tuple-element.19.power_ref), channel_id=1, source_target_pairs={{0,128},{128,0},{1,129},{129,1},{2,130},{130,2},{3,131},{131,3},{4... | collective-permute-start | bytes 24584 | tf_op jit(solution)/shard_map/ppermute | solution.py:409

commit v2 on v1

v2 whole, which is shorter than its diff:
```python
import jax
import jax.numpy as jnp
from jax import lax
from jax.experimental import pallas as pl
from jax.experimental.pallas import tpu as pltpu
from jax.sharding import Mesh
from jax.sharding import PartitionSpec as P

SEQ = ("seq_0", "seq_1")
HEAD_DIM = 64
SPAN = 256
TILE = 128
EPS = 1e-05
F32 = jnp.float32
BF16 = jnp.bfloat16


def iota(shape, dim):
    return lax.broadcasted_iota(jnp.int32, shape, dim)


def dot(a, b, ca, cb):
    return lax.dot_general(a, b, (((ca,), (cb,)), ((), ())), preferred_element_type=F32)


def exact_dot(a, b):
    return jnp.dot(a, b, precision=lax.Precision.HIGHEST, preferred_element_type=F32)


def split2(v):
    hi = v.astype(BF16)
    return hi, (v - hi.astype(F32)).astype(BF16)


def split3(v):
    hi = v.astype(BF16)
    rest = v - hi.astype(F32)
    mid = rest.astype(BF16)
    low = (rest - mid.astype(F32)).astype(BF16)
    return jnp.concatenate([hi, mid, low], axis=0)


def spread(heads, width):
    one = iota((heads, width), 0) == iota((heads, width), 1) // HEAD_DIM
    return jnp.where(one, 1.0, 0.0)


def spread3(heads, width):
    one = spread(heads, width).astype(BF16)
    return jnp.concatenate([one, one, one], axis=0)


def per_channel(v, table):
    return dot(split3(v), table, 0, 0)


def as_column(row):
    n = row.shape[1]
    return jnp.sum(jnp.where(iota((n, n), 0) == iota((n, n), 1), row, 0.0), axis=1, keepdims=True)


def as_row(column, width):
    n = column.shape[0]
    same = iota((n, width), 0) == iota((n, width), 1)
    return jnp.sum(jnp.where(same, column, 0.0), axis=0, keepdims=True)


def upper_ones(n):
    return jnp.where(iota((n, n), 0) <= iota((n, n), 1), 1.0, 0.0).astype(BF16)


def silu(v):
    return v * jax.nn.sigmoid(v)


def chosen(slots, steps):
    seqs = slots.shape[1]
    rows = steps * seqs
    seq = iota((1, rows), 1) % seqs
    takes, place = jnp.zeros((1, rows), jnp.int32), jnp.zeros((1, rows), jnp.int32)
    for d in range(seqs):
        continues = jnp.where(slots[:, d : d + 1] >= 0, 1, 0)
        takes = takes + jnp.where(seq == d, continues, 0)
        place = place + jnp.where(seq > d, continues, 0)
    shape = (steps * (seqs - 1), rows)
    row, col = iota(shape, 0), iota(shape, 1)
    same = (row % steps == col // seqs) & (row // steps == place) & (takes > 0)
    return jnp.where(same, 1.0, 0.0).astype(BF16)


def head_terms(dt_ref, rate, first, limit):
    heads, span = dt_ref.shape
    live = first + iota((heads, span), 1) < limit
    step = jnp.where(live, jax.nn.softplus(dt_ref[...].astype(F32)), 0.0)
    sums = dot(split3(-step * rate), upper_ones(span), 1, 0)
    return step, sums[:heads] + sums[heads : 2 * heads] + sums[2 * heads :]


def state_kernel(
    lengths_ref, rate_hbm, slots_hbm, dt_hbm, x_hbm, b_hbm, dec_c_hbm, out_hbm,
    rate_ref, slots_ref, dec_c_ref, dec_rows, dt, x, b, sent, sem_in, sem_out,
):
    heads, length = dt.shape
    chunks = 4
    halves = b.shape[1] // TILE
    wide = out_hbm.shape[0] // halves
    cols = x.shape[1] // chunks
    small = (
        (dt_hbm, dt), (rate_hbm, rate_ref), (dec_c_hbm, dec_c_ref), (slots_hbm, slots_ref),
        (b_hbm, b),
    )
    first = [pltpu.make_async_copy(*pair, sem_in.at[n]) for n, pair in enumerate(small)]
    loads = []
    for k in range(chunks):
        rows_at = pl.ds(k * (length // chunks), length // chunks)
        loads.append(pltpu.make_async_copy(x_hbm.at[rows_at, :], x.at[rows_at, :], sem_in.at[len(small) + k]))
    for load in (*first, *loads):
        load.start()
    for load in first[:2]:
        load.wait()
    limit = lengths_ref[0] - lax.axis_index(SEQ) * length
    live = iota((heads, length), 1) < limit
    step = jnp.where(live, jax.nn.softplus(dt[...].astype(F32)), 0.0)
    log = -step * as_column(rate_ref[...])
    spans = range(0, length, SPAN)
    stacked = jnp.concatenate([log[:, t : t + SPAN] for t in spans], axis=0)
    rows = stacked.shape[0]
    sums = dot(split3(stacked), upper_ones(SPAN), 1, 0)
    cum = sums[:rows] + sums[rows : 2 * rows] + sums[2 * rows :]
    rest = jnp.zeros((heads, 1), F32)
    weights = []
    for t in reversed(range(len(spans))):
        here = cum[t * heads : (t + 1) * heads]
        rest = rest + here[:, SPAN - 1 :]
        weights.append(step[:, t * SPAN : (t + 1) * SPAN] * jnp.exp(rest - here))
    weights = split3(jnp.concatenate(weights[::-1], axis=1))
    table = spread3(heads, chunks * cols)
    decay = per_channel(jnp.broadcast_to(jnp.exp(rest), (heads, TILE)), table)[:8]

    first[2].wait()
    first[3].wait()
    steps, seqs, _ = dec_c_ref.shape
    for s in range(steps):
        dec_rows[s * seqs : (s + 1) * seqs, :] = dec_c_ref[s].astype(F32)
    picked = dot(chosen(slots_ref[...], steps), dec_rows[...].astype(BF16), 1, 0)
    for half in range(halves):
        for col in range(wide):
            sent[half * wide + col, TILE + 8 :, :] = picked[:, half * TILE : (half + 1) * TILE]
    first[4].wait()
    b_twice = jnp.concatenate([b[...], b[...]], axis=0)
    spreads = [
        dot(weights, table[:, k * cols : (k + 1) * cols], 0, 0) for k in range(chunks)
    ]
    for load in loads:
        load.wait()
    stores = []
    for k in range(chunks):
        flow = x[:, k * cols : (k + 1) * cols].astype(F32) * spreads[k]
        state = dot(b_twice, jnp.concatenate(split2(flow), axis=0), 0, 0)
        for side in range(cols // TILE):
            col = k * (cols // TILE) + side
            for half in range(halves):
                j = half * wide + col
                at = slice(side * TILE, (side + 1) * TILE)
                sent[j, :TILE, :] = state[half * TILE : (half + 1) * TILE, at]
                sent[j, TILE : TILE + 8, :] = decay[:, col * TILE : (col + 1) * TILE]
                stores.append(pltpu.make_async_copy(sent.at[j], out_hbm.at[j], sem_out.at[j]))
                stores[-1].start()
    for store in stores:
        store.wait()


def prefix_kernel(in_ref, out_ref):
    count = in_ref.shape[0]
    dec = in_ref.shape[1] - TILE - 8
    state = jnp.zeros((TILE, TILE), F32)
    for k in range(count):
        out_ref[k, :TILE, :] = state
        state = state * in_ref[k, TILE : TILE + 1, :] + in_ref[k, :TILE, :]
    high, low = split2(state)
    c = in_ref[:, TILE + 8 :, :].reshape(count * dec, TILE).astype(BF16)
    y = dot(c, high, 1, 0) + dot(c, low, 1, 0)
    out_ref[:, TILE:, :] = y.reshape(count, dec, TILE)


def local_kernel(
    lengths_ref, rate_ref, skip_ref, dt_ref, x_ref, gate_ref, b_ref, c_ref,
    part_ref, coef_ref, state, total, skip,
):
    t = pl.program_id(0)
    heads, span = dt_ref.shape
    width = x_ref.shape[1]

    @pl.when(t == 0)
    def _():
        state[...] = jnp.zeros_like(state)
        total[...] = jnp.zeros_like(total)
        skip[...] = exact_dot(
            jnp.broadcast_to(skip_ref[...], (8, heads)), spread(heads, width)
        )

    table = spread3(heads, width)
    limit = lengths_ref[0] - lax.axis_index(SEQ) * (pl.num_programs(0) * span)
    step, cum = head_terms(dt_ref, as_column(rate_ref[...]), t * span, limit)
    last = cum[:, span - 1 :]
    b, c = b_ref[...], c_ref[...]
    x = x_ref[...].astype(F32)
    high, low = split2(x * per_channel(step * jnp.exp(-cum), table))
    lower = iota((span, span), 0) >= iota((span, span), 1)
    score_high, score_low = split2(jnp.where(lower, dot(c, b, 1, 1), 0.0))
    acc = dot(score_high, high, 1, 0) + dot(score_high, low, 1, 0) + dot(score_low, high, 1, 0)
    now = state[...]
    now_high, now_low = split2(now)
    acc = acc + dot(c, now_high, 1, 0) + dot(c, now_low, 1, 0)
    decay = per_channel(jnp.exp(cum), table)
    before = total[...]
    total[...] = before + last
    lane = iota((heads, TILE), 1)
    rows = per_channel(jnp.where(lane < 8, jnp.exp(last), jnp.exp(before)), table)
    live = t * span + iota((span, width), 0) < limit
    gate = jnp.where(live, silu(gate_ref[...].astype(F32)), 0.0)
    part_ref[...] = (acc * decay + skip[0:1] * x) * gate
    coef_ref[...] = decay * rows[8:9] * gate
    state[...] = (now + (dot(b, high, 0, 0) + dot(b, low, 0, 0))) * rows[0:1]


def decode_kernel(
    slots_ref, rate_ref, skip_ref, dt_ref, x_ref, gate_ref, b_ref, c_ref, state_ref,
    part_ref, coef_ref, x_all, gate_all, b_all, c_all, keep_log, size_all,
):
    d = pl.program_id(0)
    steps, seqs, width = x_ref.shape
    heads = dt_ref.shape[2]
    rows = steps * seqs

    @pl.when(d == 0)
    def _():
        total = jnp.zeros((seqs, heads), F32)
        for s in range(steps):
            at = pl.ds(s * seqs, seqs)
            size = jax.nn.softplus(dt_ref[s].astype(F32))
            total = total - size * rate_ref[...]
            keep_log[at, :] = total
            size_all[at, :] = size
            x_all[at, :] = x_ref[s].astype(F32)
            gate_all[at, :] = gate_ref[s].astype(F32)
            b_all[at, :] = b_ref[s].astype(F32)
            c_all[at, :] = c_ref[s].astype(F32)
        table = spread(heads, width)
        keep = exact_dot(jnp.exp(keep_log[...]), table)
        flow = exact_dot(size_all[...] * jnp.exp(-keep_log[...]), table) * x_all[...]
        scores = dot(c_all[...].astype(BF16), b_all[...].astype(BF16), 1, 1)
        row, col = iota((rows, rows), 0), iota((rows, rows), 1)
        same = (row % seqs == col % seqs) & (col <= row)
        inner = exact_dot(jnp.where(same, scores, 0.0), flow)
        skip = exact_dot(jnp.broadcast_to(skip_ref[...], (8, heads)), table)[0:1]
        gate = silu(gate_all[...])
        part_ref[...] = (keep * inner + skip * x_all[...]) * gate
        coef_ref[...] = keep * gate

    c = c_all[...].astype(BF16)
    high, low = split2(state_ref[0])
    own = dot(c, high, 1, 1) + dot(c, low, 1, 1)
    mine = iota((rows, 1), 0) % seqs == d
    take = mine & (slots_ref[d] < 0)
    part_ref[...] += jnp.where(take, own * coef_ref[...], 0.0)
    coef_ref[...] = jnp.where(take, 0.0, coef_ref[...])


def mix_kernel(
    coef_hbm, slots_ref, in_ref, c_ref, part_ref, dec_part_ref, dec_coef_ref,
    mixed_ref, dec_mixed_ref, power_ref, coef, sem,
):
    length, width = part_ref.shape
    loads = []
    for t in range(length // SPAN):
        at = pl.ds(t * SPAN, SPAN)
        loads.append(pltpu.make_async_copy(coef_hbm.at[at, :], coef.at[at, :], sem.at[t]))
        loads[-1].start()
    wide = width // TILE
    halves = in_ref.shape[0] // wide
    pieces = [
        jnp.concatenate([in_ref[h * wide + col, :TILE, :] for h in range(halves)], axis=0)
        for col in range(wide)
    ]
    twice = jnp.concatenate(split2(jnp.concatenate(pieces, axis=1)), axis=0)
    final = jnp.concatenate(
        [in_ref[col, TILE:, :] + in_ref[wide + col, TILE:, :] for col in range(wide)], axis=1
    )
    steps = final.shape[0] // (slots_ref.shape[1] - 1)
    picks = chosen(slots_ref[...], steps)
    final = dot(jnp.concatenate([picks] * 3, axis=0), split3(final), 0, 0)
    dec_mixed = dec_part_ref[...] + dec_coef_ref[...] * final
    dec_mixed_ref[...] = dec_mixed
    power = jnp.sum(dec_mixed * dec_mixed, axis=1, keepdims=True)
    power_ref[...] = jnp.zeros_like(power_ref)
    power_ref[4:5, :] = as_row(power, SPAN)
    for t in range(length // SPAN):
        at = slice(t * SPAN, (t + 1) * SPAN)
        c = c_ref[at, :]
        from_before = dot(jnp.concatenate([c, c], axis=1), twice, 1, 0)
        loads[t].wait()
        mixed = part_ref[at, :] + coef[at, :] * from_before
        mixed_ref[at, :] = mixed
        power_ref[t : t + 1, :] = as_row(jnp.sum(mixed * mixed, axis=1, keepdims=True), SPAN)


def norm_kernel(
    power_ref, other_ref, gain_ref, mixed_ref, dec_mixed_ref, out_hbm, dec_ref, out, dec, sem
):
    length, width = mixed_ref.shape
    scales = lax.rsqrt((power_ref[...] + other_ref[...]) / (2 * width) + EPS)
    stores = []
    for t in range(length // SPAN):
        at = pl.ds(t * SPAN, SPAN)
        out[at, :] = (mixed_ref[at, :] * as_column(scales[t : t + 1]) * gain_ref[...]).astype(BF16)
        stores.append(pltpu.make_async_copy(out.at[at, :], out_hbm.at[at, :], sem.at[t]))
        stores[-1].start()
    steps, seqs, _ = dec_ref.shape
    rows = steps * seqs
    dec[...] = dec_mixed_ref[...] * as_column(scales[4:5, :TILE])[:rows] * gain_ref[...]
    for s in range(steps):
        dec_ref[s] = dec[s * seqs : (s + 1) * seqs, :].astype(BF16)
    for store in stores:
        store.wait()


def params(mib):
    return pltpu.CompilerParams(
        dimension_semantics=("arbitrary",), vmem_limit_bytes=mib * 2**20
    )


def whole(shape):
    return pl.BlockSpec(shape, lambda t: (0,) * len(shape))


def by_rows(shape):
    return pl.BlockSpec(shape, lambda t: (t,) + (0,) * (len(shape) - 1))


def in_hbm(v):
    return pltpu.with_memory_space_constraint(v, pltpu.HBM)


def in_vmem(v):
    return pltpu.with_memory_space_constraint(v, pltpu.VMEM)


HBM = pl.BlockSpec(memory_space=pltpu.HBM)
VMEM = pl.BlockSpec(memory_space=pltpu.VMEM)
SMEM = pl.BlockSpec(memory_space=pltpu.SMEM)


def cost(flops, mib):
    return pl.CostEstimate(flops=flops, bytes_accessed=mib * 2**20, transcendentals=0)


def device_state(lengths, rate, slots, dt, x, b, dec_c, count):
    heads, length = dt.shape
    state, width = b.shape[1], x.shape[1]
    steps, seqs, _ = dec_c.shape
    shape = (count, TILE + 8 + steps * (seqs - 1), TILE)
    return pl.pallas_call(
        state_kernel,
        name="device_state",
        out_shape=pltpu.HBM(shape, F32),
        in_specs=[SMEM] + [HBM] * 6,
        out_specs=HBM,
        scratch_shapes=[
            pltpu.VMEM(rate.shape, F32),
            pltpu.VMEM(slots.shape, jnp.int32),
            pltpu.VMEM(dec_c.shape, BF16),
            pltpu.VMEM((steps * seqs, state), F32),
            pltpu.VMEM((heads, length), BF16),
            pltpu.VMEM((length, width), BF16),
            pltpu.VMEM((length, state), BF16),
            pltpu.VMEM(shape, F32),
            pltpu.SemaphoreType.DMA((9,)),
            pltpu.SemaphoreType.DMA((count,)),
        ],
        compiler_params=pltpu.CompilerParams(vmem_limit_bytes=48 * 2**20),
        cost_estimate=cost(8 * length * state * width, 6),
    )(lengths, *map(in_hbm, (rate, slots, dt, x, b, dec_c)))


def device_outputs(lengths, rate, skip, dt, x, gate, b, c):
    heads, length = dt.shape
    state, width = b.shape[1], x.shape[1]
    wide_spec, state_spec = by_rows((SPAN, width)), by_rows((SPAN, state))
    head_spec = whole((1, heads))
    return pl.pallas_call(
        local_kernel,
        name="device_outputs",
        out_shape=[pltpu.HBM((length, width), F32)] * 2,
        grid=(length // SPAN,),
        in_specs=[
            SMEM, head_spec, head_spec, pl.BlockSpec((heads, SPAN), lambda t: (0, t)),
            wide_spec, wide_spec, state_spec, state_spec,
        ],
        out_specs=[wide_spec, wide_spec],
        scratch_shapes=[
            pltpu.VMEM((state, width), F32),
            pltpu.VMEM((heads, TILE), F32),
            pltpu.VMEM((8, width), F32),
        ],
        compiler_params=params(32),
        cost_estimate=cost(20 * length * state * width, 14),
    )(lengths, *map(in_hbm, (rate, skip, dt, x, gate, b, c)))


def decode_own(slots, rate, skip, dt, x, gate, b, c, states):
    steps, seqs, width = x.shape
    heads, state, rows = dt.shape[2], b.shape[2], steps * seqs
    return pl.pallas_call(
        decode_kernel,
        name="decode_own",
        out_shape=[jax.ShapeDtypeStruct((rows, width), F32)] * 2,
        grid=(seqs,),
        in_specs=[
            SMEM, whole((1, heads)), whole((1, heads)), whole((steps, seqs, heads)),
            whole((steps, seqs, width)), whole((steps, seqs, width)),
            whole((steps, seqs, state)), whole((steps, seqs, state)),
            by_rows((1, width, state)),
        ],
        out_specs=[whole((rows, width))] * 2,
        scratch_shapes=[
            pltpu.VMEM((rows, width), F32), pltpu.VMEM((rows, width), F32),
            pltpu.VMEM((rows, state), F32), pltpu.VMEM((rows, state), F32),
            pltpu.VMEM((rows, heads), F32), pltpu.VMEM((rows, heads), F32),
        ],
        compiler_params=params(16),
        cost_estimate=cost(4 * seqs * 256 * state * width, 5),
    )(slots, *map(in_hbm, (rate, skip, dt, x, gate, b, c, states)))


def prefix(owned):
    count, rows, _ = owned.shape
    return pl.pallas_call(
        prefix_kernel,
        name="prefix",
        out_shape=jax.ShapeDtypeStruct((count, rows - 8, TILE), F32),
        compiler_params=pltpu.CompilerParams(vmem_limit_bytes=16 * 2**20),
        cost_estimate=cost(2 * count * 32 * TILE * TILE, 3),
    )(owned)


def mix(coef, slots, entry, c, part, dec_part, dec_coef):
    length, width = part.shape
    return pl.pallas_call(
        mix_kernel,
        name="mix",
        out_shape=[
            pltpu.VMEM((length, width), F32),
            pltpu.VMEM(dec_part.shape, F32),
            pltpu.VMEM((8, SPAN), F32),
        ],
        in_specs=[HBM] + [VMEM] * 6,
        out_specs=[VMEM] * 3,
        scratch_shapes=[
            pltpu.VMEM((length, width), F32), pltpu.SemaphoreType.DMA((length // SPAN,)),
        ],
        compiler_params=pltpu.CompilerParams(vmem_limit_bytes=32 * 2**20),
        cost_estimate=cost(4 * length * c.shape[1] * width, 14),
    )(in_hbm(coef), slots, entry, c, part, dec_part, dec_coef)


def norm(power, other, gain, mixed, dec_mixed, dec_shape):
    length, width = mixed.shape
    return pl.pallas_call(
        norm_kernel,
        name="norm",
        out_shape=[pltpu.HBM((length, width), BF16), jax.ShapeDtypeStruct(dec_shape, BF16)],
        in_specs=[VMEM] * 5,
        out_specs=[HBM, VMEM],
        scratch_shapes=[
            pltpu.VMEM((length, width), BF16),
            pltpu.VMEM(dec_mixed.shape, F32),
            pltpu.SemaphoreType.DMA((length // SPAN,)),
        ],
        compiler_params=pltpu.CompilerParams(vmem_limit_bytes=16 * 2**20),
        cost_estimate=cost(4 * length * width, 6),
    )(power, other, gain, mixed, dec_mixed)


def shards(
    x_in, gate_in, dt_raw, b_in, c_in, lengths, decay_rate, skip_gain, norm_gain,
    dec_states, dec_x, dec_gate, dec_dt, dec_b, dec_c, slots,
):
    _, length, _, width = x_in.shape
    heads, state = dt_raw.shape[3], b_in.shape[3]
    steps, seqs = dec_x.shape[:2]
    count = lax.axis_size(SEQ)
    x, gate = x_in.reshape(length, width), gate_in.reshape(length, width)
    dt = dt_raw.reshape(length, heads).T
    b, c = b_in.reshape(length, state), c_in.reshape(length, state)
    dec_x, dec_gate = dec_x.reshape(steps, seqs, width), dec_gate.reshape(steps, seqs, width)
    dec_b, dec_c = dec_b.reshape(steps, seqs, state), dec_c.reshape(steps, seqs, state)
    dec_dt = dec_dt.reshape(steps, seqs, heads)

    slots_row = slots.reshape(1, seqs)
    sent = device_state(lengths, decay_rate, slots_row, dt, x, b, dec_c, count)
    owned = lax.all_to_all(sent, SEQ, 0, 0)
    part, coef = device_outputs(lengths, decay_rate, skip_gain, dt, x, gate, b, c)
    dec_part, dec_coef = decode_own(
        slots, decay_rate, skip_gain, dec_dt, dec_x, dec_gate, dec_b, dec_c,
        dec_states.reshape(seqs, width, state),
    )
    owned, part, coef, dec_part, dec_coef = lax.optimization_barrier(
        (owned, part, coef, dec_part, dec_coef)
    )
    entry = lax.all_to_all(prefix(owned), SEQ, 0, 0)
    mixed, dec_mixed, power = mix(coef, slots_row, entry, c, part, dec_part, dec_coef)
    other = lax.ppermute(power, "pool", [(0, 1), (1, 0)])
    prefill_out, decode_out = norm(
        power, other, norm_gain, mixed, dec_mixed, (steps, seqs, width)
    )
    return prefill_out.reshape(x_in.shape), decode_out.reshape(steps, seqs, 1, width)


def solution(mesh):
    split = Mesh(
        mesh.devices.reshape(mesh.shape["pool"], 4, 4, mesh.shape["head"]),
        ("pool", "seq_0", "seq_1", "head"),
    )
    wide = P(None, SEQ, "head", "pool")
    shared = P(None, SEQ, "head", None)
    per_head = P("head", "pool")
    return jax.shard_map(
        shards,
        mesh=split,
        in_specs=(
            wide, wide, wide, shared, shared, P(), per_head, per_head, per_head,
            P(SEQ, "head", "pool", None, None), wide, wide, wide, shared, shared, P(SEQ),
        ),
        out_specs=(wide, wide),
        check_vma=False,
    )
```

time: 68.7 us -> 63.3 us (0.921)
  Pallas kernels: 31 us -> 26.4 us
    pallas_call x6, Pallas kernels: 31 us -> 26.4 us  [the longest x1 11.5 us: device_outputs(): pl.pallas_call(local_kernel, name='device_outputs', out_shape=[pltpu.HBM(...]
  transfers between devices with their start and end apart: 2 -> 2, of which waited for: 2 -> 2; matrix products, arithmetic and copies ran while one was open for 0% -> 0% of each run, Pallas kernels for 24% -> 26%
where the time goes in v2:
time: 63.3 us; the launch traced here: 63 us
  Pallas kernels  26.4 us (42%)
  blocking collectives  21.2 us (33%)
  starting transfers between devices  11.3 us (18%)
  waiting for transfers between devices  2.76 us (4%)
  between operations  1.34 us (2%)
    all_to_all x1, blocking collectives, shards(): entry = lax.all_to_all(prefix(owned), SEQ, 0, 0)  21.2 us
    pallas_call x1, Pallas kernels, device_outputs(): pl.pallas_call(local_kernel, name='device_outputs', out_shape=[pltpu.HBM(...  11.5 us
    all_to_all x1, starting transfers between devices, shards(): owned = lax.all_to_all(sent, SEQ, 0, 0)  7.59 us
    pallas_call x1, Pallas kernels, device_state(): pl.pallas_call(state_kernel, name='device_state', out_shape=pltpu.HBM(sha...  4.71 us
    pallas_call x1, Pallas kernels, decode_own(): pl.pallas_call(decode_kernel, name='decode_own', out_shape=[jax.ShapeDtyp...  4.6 us
    ppermute x1, starting transfers between devices, shards(): other = lax.ppermute(power, 'pool', [(0, 1), (1, 0)])  3.74 us
    pallas_call x1, Pallas kernels, mix(): pl.pallas_call(mix_kernel, name='mix', out_shape=[pltpu.VMEM((length, wid...  3.11 us
    pallas_call x1, Pallas kernels, norm(): pl.pallas_call(norm_kernel, name='norm', out_shape=[pltpu.HBM((length, wi...  2.16 us
  transfers between devices with their start and end apart: 2, of which 2 were waited for; matrix products, arithmetic and copies ran while one was open for 0% of the time, Pallas kernels for 26%

profile of v2, /device:TPU:1, one launch (start us, length us, event | category | flops | bytes accessed | tf_op | source)
XLA Modules:
  0.0 63.0 jit_solution(11898809059547723397)
XLA Ops:
  1.3 4.7 %device_state.1 = f32[16,160,128]{2,1,0:T(8,128)} custom-call(s32[1]{0:T(128)S(6)} %copy.19.lengths_ref, f32[1,16]{1,0:T(1,128)} %rate_ref.3, s32[1,4]{1,0:T(1,128)} %bitcast.20, bf16[16,1024]{1,0:T(8,128)(2,1)} %bitcast.36, bf16[1024,1024]{1,0:T(8,128)(2,1)} %bitcast.29, bf16[1024,256]{1,0:T(8,128)(2,1)} %bitcast.33, bf16[8,4,256]{2,1,0:T(4,128)(2,1)} %bitcast.25), custom_call_target="tpu_custom_call" | custom-call | flops 2147483648 | bytes 6291456 | tf_op jit(solution)/shard_map/device_state/pallas_call | solution.py:364
  6.0 0.0 copy-start.3
  6.0 7.6 %all-to-all-start = ((f32[16,160,128]{2,1,0:T(8,128)}), f32[16,160,128]{2,1,0:T(8,128)S(1)}, u32[]{:S(2)}, u32[]{:S(2)}) async-start(f32[16,160,128]{2,1,0:T(8,128)} %device_state.1), calls=%async_computation | async-start | bytes 2621440 | tf_op jit(solution)/shard_map/all_to_all | solution.py:503
  13.6 0.0 copy-done.3
  13.6 4.6 %decode_own.1 = (f32[32,1024]{1,0:T(8,128)S(1)}, f32[32,1024]{1,0:T(8,128)S(1)}) custom-call(s32[4]{0:T(128)S(1)} %copy-done.3, f32[1,16]{1,0:T(1,128)} %rate_ref.3, f32[1,16]{1,0:T(1,128)} %skip_ref.3, bf16[8,4,16]{2,1,0:T(4,128)(2,1)} %bitcast.28, bf16[8,4,1024]{2,1,0:T(4,128)(2,1)} %bitcast.23, bf16[8,4,1024]{2,1,0:T(4,128)(2,1)} %bitcast.24, ...), custom_call_target="tpu_custom_call" | custom-call | flops 1073741824 | bytes 5242880 | tf_op jit(solution)/shard_map/decode_own/pallas_call | solution.py:415
  18.2 11.5 %device_outputs.1 = (f32[1024,1024]{1,0:T(8,128)}, f32[1024,1024]{1,0:T(8,128)}) custom-call(s32[1]{0:T(128)S(6)} %copy.19.lengths_ref, f32[1,16]{1,0:T(1,128)} %rate_ref.3, f32[1,16]{1,0:T(1,128)} %skip_ref.3, bf16[16,1024]{1,0:T(8,128)(2,1)} %bitcast.37, bf16[1024,1024]{1,0:T(8,128)(2,1)} %bitcast.30, bf16[1024,1024]{1,0:T(8,128)(2,1)} %bitcast.31, ...), custom_call_target="tpu_custom_call" | custom-call | flops 5368709120 | bytes 14680064 | tf_op jit(solution)/shard_map/device_outputs/pallas_call | solution.py:392
  29.7 1.9 %all-to-all-done.in_ref = f32[16,160,128]{2,1,0:T(8,128)S(1)} async-done(((f32[16,160,128]{2,1,0:T(8,128)}), f32[16,160,128]{2,1,0:T(8,128)S(1)}, u32[]{:S(2)}, u32[]{:S(2)}) %all-to-all-start) | async-done | bytes 1310752 | tf_op jit(solution)/shard_map/all_to_all | solution.py:503
  31.7 0.0 copy-start
  31.7 0.0 copy-start.1
  31.7 0.3 prefix.1
  32.0 21.2 %all_to_all.10.in_ref = f32[16,152,128]{2,1,0:T(8,128)S(1)} all-to-all(f32[16,152,128]{2,1,0:T(8,128)S(1)} %prefix.1), channel_id=1, replica_groups=mesh['pool'=2,'seq_0'=4,'seq_1'=4,'head'=8] {'seq_0','seq_1'}, dimensions={0} | all-to-all | bytes 2490368 | tf_op jit(solution)/shard_map/all_to_all | solution.py:512
  53.1 0.0 copy-done
  53.1 0.0 copy-done.1
  53.1 0.0 copy-start.2
  53.1 3.1 %mix.1 = (f32[1024,1024]{1,0:T(8,128)S(1)}, f32[32,1024]{1,0:T(8,128)S(1)}, f32[8,256]{1,0:T(8,128)S(1)}) custom-call(f32[1024,1024]{1,0:T(8,128)} %get-tuple-element.20.coef_hbm, s32[1,4]{1,0:T(1,128)S(1)} %bitcast.21, f32[16,152,128]{2,1,0:T(8,128)S(1)} %all_to_all.10.in_ref, bf16[1024,256]{1,0:T(8,128)(2,1)S(1)} %bitcast.19, f32[1024,1024]{1,0:T(8,128)S(1)} %copy-done, ...), custom_call_target="tpu_custom_call" | custom-call | flops 1073741824 | bytes 14680064 | tf_op jit(solution)/shard_map/mix/pallas_call | solution.py:450
  56.3 3.7 %collective-permute-start = (f32[8,256]{1,0:T(8,128)S(1)}, f32[8,256]{1,0:T(8,128)S(1)}, u32[]{:S(2)}, u32[]{:S(2)}) collective-permute-start(f32[8,256]{1,0:T(8,128)S(1)} %get-tuple-element.25.power_ref), channel_id=1, source_target_pairs={{0,128},{128,0},{1,129},{129,1},{2,130},{130,2},{3,131},{131,3},{4... | collective-permute-start | bytes 24584 | tf_op jit(solution)/shard_map/ppermute | solution.py:514
  60.0 0.8 %collective-permute-done.other_ref = f32[8,256]{1,0:T(8,128)S(1)} collective-permute-done((f32[8,256]{1,0:T(8,128)S(1)}, f32[8,256]{1,0:T(8,128)S(1)}, u32[]{:S(2)}, u32[]{:S(2)}) %collective-permute-start) | collective-permute-done | bytes 8224 | tf_op jit(solution)/shard_map/ppermute | solution.py:514
  60.8 0.0 copy-done.2
  60.8 2.2 %norm.1 = (bf16[1024,1024]{1,0:T(8,128)(2,1)}, bf16[8,4,1024]{2,1,0:T(4,128)(2,1)}) custom-call(f32[8,256]{1,0:T(8,128)S(1)} %get-tuple-element.25.power_ref, f32[8,256]{1,0:T(8,128)S(1)} %collective-permute-done.other_ref, f32[1,1024]{1,0:T(1,128)S(1)} %copy-done.2, f32[1024,1024]{1,0:T(8,128)S(1)} %get-tuple-element.26.mixed_ref, ...), custom_call_target="tpu_custom_call" | custom-call | flops 4194304 | bytes 6291456 | tf_op jit(solution)/shard_map/norm/pallas_call | solution.py:470
Async XLA Ops:
  6.0 7.6 %copy-start.3 = (s32[4]{0:T(128)S(1)}, s32[4]{0:T(128)}, u32[]{:S(2)}) copy-start(s32[4]{0:T(128)} %slots_ref.1) | copy-start | bytes 52
  6.0 25.7 %all-to-all-start = ((f32[16,160,128]{2,1,0:T(8,128)}), f32[16,160,128]{2,1,0:T(8,128)S(1)}, u32[]{:S(2)}, u32[]{:S(2)}) async-start(f32[16,160,128]{2,1,0:T(8,128)} %device_state.1), calls=%async_computation | async-start | bytes 2621440 | tf_op jit(solution)/shard_map/all_to_all | solution.py:503
  31.7 21.4 %copy-start = (f32[1024,1024]{1,0:T(8,128)S(1)}, f32[1024,1024]{1,0:T(8,128)}, u32[]{:S(2)}) copy-start(f32[1024,1024]{1,0:T(8,128)} %get-tuple-element.22.part_ref) | copy-start | bytes 12582916
  31.7 21.4 %copy-start.1 = (bf16[1,1024,1,256]{3,1,2,0:T(8,128)(2,1)S(1)}, bf16[1,1024,1,256]{3,1,2,0:T(8,128)(2,1)}, u32[]{:S(2)}) copy-start(bf16[1,1024,1,256]{3,1,2,0:T(8,128)(2,1)} %param.20) | copy-start | bytes 1572868
  53.1 7.7 %copy-start.2 = (f32[1,1024]{1,0:T(1,128)S(1)}, f32[1,1024]{1,0:T(1,128)}, u32[]{:S(2)}) copy-start(f32[1,1024]{1,0:T(1,128)} %gain_ref.1) | copy-start | bytes 12292
  56.3 4.6 %collective-permute-start = (f32[8,256]{1,0:T(8,128)S(1)}, f32[8,256]{1,0:T(8,128)S(1)}, u32[]{:S(2)}, u32[]{:S(2)}) collective-permute-start(f32[8,256]{1,0:T(8,128)S(1)} %get-tuple-element.25.power_ref), channel_id=1, source_target_pairs={{0,128},{128,0},{1,129},{129,1},{2,130},{130,2},{3,131},{131,3},{4... | collective-permute-start | bytes 24584 | tf_op jit(solution)/shard_map/ppermute | solution.py:514

commit v3 on v2

--- a/solution.py
+++ b/solution.py
@@ -1,3 +1,5 @@
+import functools
+
 import jax
 import jax.numpy as jnp
 from jax import lax
@@ -97,7 +99,7 @@
 
 
 def state_kernel(
-    lengths_ref, rate_hbm, slots_hbm, dt_hbm, x_hbm, b_hbm, dec_c_hbm, out_hbm,
+    lengths_ref, rate_hbm, slots_hbm, dt_hbm, x_hbm, b_hbm, dec_c_hbm, _, out_hbm,
     rate_ref, slots_ref, dec_c_ref, dec_rows, dt, x, b, sent, sem_in, sem_out,
 ):
     heads, length = dt.shape
@@ -137,8 +139,11 @@
     table = spread3(heads, chunks * cols)
     decay = per_channel(jnp.broadcast_to(jnp.exp(rest), (heads, TILE)), table)[:8]
 
-    first[2].wait()
-    first[3].wait()
+    spreads = [
+        dot(weights, table[:, k * cols : (k + 1) * cols], 0, 0) for k in range(chunks)
+    ]
+    for load in (*first[2:], *loads):
+        load.wait()
     steps, seqs, _ = dec_c_ref.shape
     for s in range(steps):
         dec_rows[s * seqs : (s + 1) * seqs, :] = dec_c_ref[s].astype(F32)
@@ -146,13 +151,7 @@
     for half in range(halves):
         for col in range(wide):
             sent[half * wide + col, TILE + 8 :, :] = picked[:, half * TILE : (half + 1) * TILE]
-    first[4].wait()
     b_twice = jnp.concatenate([b[...], b[...]], axis=0)
-    spreads = [
-        dot(weights, table[:, k * cols : (k + 1) * cols], 0, 0) for k in range(chunks)
-    ]
-    for load in loads:
-        load.wait()
     stores = []
     for k in range(chunks):
         flow = x[:, k * cols : (k + 1) * cols].astype(F32) * spreads[k]
@@ -224,59 +223,92 @@
     state[...] = (now + (dot(b, high, 0, 0) + dot(b, low, 0, 0))) * rows[0:1]
 
 
-def decode_kernel(
-    slots_ref, rate_ref, skip_ref, dt_ref, x_ref, gate_ref, b_ref, c_ref, state_ref,
-    part_ref, coef_ref, x_all, gate_all, b_all, c_all, keep_log, size_all,
+def decode_kernel(turn, *refs):
+    part_hbm, coef_hbm = refs[9:11]
+    work, (part, coef, sem), store_sem = refs[11:-4], refs[-4:-1], refs[-1]
+
+    @pl.when(lax.axis_index("pool") == turn)
+    def _():
+        decode_work(*refs[:9], *work, part, coef, sem)
+        pairs = ((part, part_hbm), (coef, coef_hbm))
+        stores = [pltpu.make_async_copy(*p, store_sem.at[n]) for n, p in enumerate(pairs)]
+        for store in stores:
+            store.start()
+        for store in stores:
+            store.wait()
+
+
+def decode_work(
+    slots_hbm, rate_hbm, skip_hbm, dt_hbm, x_hbm, gate_hbm, b_hbm, c_hbm, states_hbm,
+    slots_ref, rate_ref, skip_ref, dt_ref, x_ref, gate_ref, b_ref, c_ref, states,
+    x_all, gate_all, b_all, c_all, keep_log, size_all, part, coef, sem,
 ):
-    d = pl.program_id(0)
     steps, seqs, width = x_ref.shape
     heads = dt_ref.shape[2]
     rows = steps * seqs
-
-    @pl.when(d == 0)
-    def _():
-        total = jnp.zeros((seqs, heads), F32)
-        for s in range(steps):
-            at = pl.ds(s * seqs, seqs)
-            size = jax.nn.softplus(dt_ref[s].astype(F32))
-            total = total - size * rate_ref[...]
-            keep_log[at, :] = total
-            size_all[at, :] = size
-            x_all[at, :] = x_ref[s].astype(F32)
-            gate_all[at, :] = gate_ref[s].astype(F32)
-            b_all[at, :] = b_ref[s].astype(F32)
-            c_all[at, :] = c_ref[s].astype(F32)
-        table = spread(heads, width)
-        keep = exact_dot(jnp.exp(keep_log[...]), table)
-        flow = exact_dot(size_all[...] * jnp.exp(-keep_log[...]), table) * x_all[...]
-        scores = dot(c_all[...].astype(BF16), b_all[...].astype(BF16), 1, 1)
-        row, col = iota((rows, rows), 0), iota((rows, rows), 1)
-        same = (row % seqs == col % seqs) & (col <= row)
-        inner = exact_dot(jnp.where(same, scores, 0.0), flow)
-        skip = exact_dot(jnp.broadcast_to(skip_ref[...], (8, heads)), table)[0:1]
-        gate = silu(gate_all[...])
-        part_ref[...] = (keep * inner + skip * x_all[...]) * gate
-        coef_ref[...] = keep * gate
-
+    pairs = (
+        (slots_hbm, slots_ref), (rate_hbm, rate_ref), (skip_hbm, skip_ref), (dt_hbm, dt_ref),
+        (x_hbm, x_ref), (gate_hbm, gate_ref), (b_hbm, b_ref), (c_hbm, c_ref),
+        (states_hbm, states),
+    )
+    loads = [pltpu.make_async_copy(*pair, sem.at[n]) for n, pair in enumerate(pairs)]
+    for load in loads:
+        load.start()
+    for load in loads[:-1]:
+        load.wait()
+    total = jnp.zeros((seqs, heads), F32)
+    for s in range(steps):
+        at = pl.ds(s * seqs, seqs)
+        size = jax.nn.softplus(dt_ref[s].astype(F32))
+        total = total - size * rate_ref[...]
+        keep_log[at, :] = total
+        size_all[at, :] = size
+        x_all[at, :] = x_ref[s].astype(F32)
+        gate_all[at, :] = gate_ref[s].astype(F32)
+        b_all[at, :] = b_ref[s].astype(F32)
+        c_all[at, :] = c_ref[s].astype(F32)
+    table = spread(heads, width)
+    keep = exact_dot(jnp.exp(keep_log[...]), table)
+    flow = exact_dot(size_all[...] * jnp.exp(-keep_log[...]), table) * x_all[...]
     c = c_all[...].astype(BF16)
-    high, low = split2(state_ref[0])
-    own = dot(c, high, 1, 1) + dot(c, low, 1, 1)
-    mine = iota((rows, 1), 0) % seqs == d
-    take = mine & (slots_ref[d] < 0)
-    part_ref[...] += jnp.where(take, own * coef_ref[...], 0.0)
-    coef_ref[...] = jnp.where(take, 0.0, coef_ref[...])
-
-
-def mix_kernel(
-    coef_hbm, slots_ref, in_ref, c_ref, part_ref, dec_part_ref, dec_coef_ref,
-    mixed_ref, dec_mixed_ref, power_ref, coef, sem,
-):
+    scores = dot(c, b_all[...].astype(BF16), 1, 1)
+    row, col = iota((rows, rows), 0), iota((rows, rows), 1)
+    same = (row % seqs == col % seqs) & (col <= row)
+    inner = exact_dot(jnp.where(same, scores, 0.0), flow)
+    skip = exact_dot(jnp.broadcast_to(skip_ref[...], (8, heads)), table)[0:1]
+    gate = silu(gate_all[...])
+    seq = iota((rows, 1), 0) % seqs
+    loads[-1].wait()
+    own = jnp.zeros((rows, width), F32)
+    keeps = jnp.zeros((rows, 1), jnp.int32)
+    for d in range(seqs):
+        high, low = split2(states[d])
+        mine = (seq == d) & (slots_ref[:, d : d + 1] < 0)
+        own = jnp.where(mine, dot(c, high, 1, 1) + dot(c, low, 1, 1), own)
+        keeps = jnp.where(mine, 1, keeps)
+    part[...] = (keep * (inner + own) + skip * x_all[...]) * gate
+    coef[...] = jnp.where(keeps > 0, 0.0, keep * gate)
+
+
+def mix_kernel(turn, *refs):
+    decode, refs = refs[:9], refs[9:]
+    coef_hbm, dec_part_hbm, dec_coef_hbm, slots_ref, in_ref, c_ref, part_ref = refs[:7]
+    mixed_ref, dec_mixed_ref, power_ref, coef, sem, *work = refs[7:]
+    dec_part, dec_coef = work[-3:-1]
     length, width = part_ref.shape
     loads = []
     for t in range(length // SPAN):
         at = pl.ds(t * SPAN, SPAN)
         loads.append(pltpu.make_async_copy(coef_hbm.at[at, :], coef.at[at, :], sem.at[t]))
         loads[-1].start()
+    pairs = ((dec_part_hbm, dec_part), (dec_coef_hbm, dec_coef))
+    done = [pltpu.make_async_copy(*p, sem.at[len(loads) + n]) for n, p in enumerate(pairs)]
+
+    @pl.when(lax.axis_index("pool") != turn)
+    def _():
+        for load in done:
+            load.start()
+
     wide = width // TILE
     halves = in_ref.shape[0] // wide
     pieces = [
@@ -284,25 +316,46 @@
         for col in range(wide)
     ]
     twice = jnp.concatenate(split2(jnp.concatenate(pieces, axis=1)), axis=0)
+    power_ref[...] = jnp.zeros_like(power_ref)
+    spans = length // SPAN
+
+    def carried(t):
+        c = c_ref[t * SPAN : (t + 1) * SPAN, :]
+        return dot(jnp.concatenate([c, c], axis=1), twice, 1, 0)
+
+    each = spans // 2
+    ready = [carried(t) for t in range(each)]
+    for k in range(2):
+        now = ready
+        for load in loads[k * each : (k + 1) * each]:
+            load.wait()
+        if k + 1 < 2:
+            ready = [carried(t) for t in range((k + 1) * each, (k + 2) * each)]
+        for t in range(k * each, (k + 1) * each):
+            at = slice(t * SPAN, (t + 1) * SPAN)
+            mixed = part_ref[at, :] + coef[at, :] * now[t - k * each]
+            mixed_ref[at, :] = mixed
+            power_ref[t : t + 1, :] = as_row(jnp.sum(mixed * mixed, axis=1, keepdims=True), SPAN)
+
+    @pl.when(lax.axis_index("pool") != turn)
+    def _():
+        for load in done:
+            load.wait()
+
+    @pl.when(lax.axis_index("pool") == turn)
+    def _():
+        decode_work(*decode, *work)
+
     final = jnp.concatenate(
         [in_ref[col, TILE:, :] + in_ref[wide + col, TILE:, :] for col in range(wide)], axis=1
     )
     steps = final.shape[0] // (slots_ref.shape[1] - 1)
     picks = chosen(slots_ref[...], steps)
     final = dot(jnp.concatenate([picks] * 3, axis=0), split3(final), 0, 0)
-    dec_mixed = dec_part_ref[...] + dec_coef_ref[...] * final
+    dec_mixed = dec_part[...] + dec_coef[...] * final
     dec_mixed_ref[...] = dec_mixed
     power = jnp.sum(dec_mixed * dec_mixed, axis=1, keepdims=True)
-    power_ref[...] = jnp.zeros_like(power_ref)
     power_ref[4:5, :] = as_row(power, SPAN)
-    for t in range(length // SPAN):
-        at = slice(t * SPAN, (t + 1) * SPAN)
-        c = c_ref[at, :]
-        from_before = dot(jnp.concatenate([c, c], axis=1), twice, 1, 0)
-        loads[t].wait()
-        mixed = part_ref[at, :] + coef[at, :] * from_before
-        mixed_ref[at, :] = mixed
-        power_ref[t : t + 1, :] = as_row(jnp.sum(mixed * mixed, axis=1, keepdims=True), SPAN)
 
 
 def norm_kernel(
@@ -356,7 +409,7 @@
     return pl.CostEstimate(flops=flops, bytes_accessed=mib * 2**20, transcendentals=0)
 
 
-def device_state(lengths, rate, slots, dt, x, b, dec_c, count):
+def device_state(lengths, rate, slots, dt, x, b, dec_c, after, count):
     heads, length = dt.shape
     state, width = b.shape[1], x.shape[1]
     steps, seqs, _ = dec_c.shape
@@ -365,7 +418,7 @@
         state_kernel,
         name="device_state",
         out_shape=pltpu.HBM(shape, F32),
-        in_specs=[SMEM] + [HBM] * 6,
+        in_specs=[SMEM] + [HBM] * 7,
         out_specs=HBM,
         scratch_shapes=[
             pltpu.VMEM(rate.shape, F32),
@@ -381,7 +434,7 @@
         ],
         compiler_params=pltpu.CompilerParams(vmem_limit_bytes=48 * 2**20),
         cost_estimate=cost(8 * length * state * width, 6),
-    )(lengths, *map(in_hbm, (rate, slots, dt, x, b, dec_c)))
+    )(lengths, *map(in_hbm, (rate, slots, dt, x, b, dec_c, after)))
 
 
 def device_outputs(lengths, rate, skip, dt, x, gate, b, c):
@@ -409,29 +462,30 @@
     )(lengths, *map(in_hbm, (rate, skip, dt, x, gate, b, c)))
 
 
-def decode_own(slots, rate, skip, dt, x, gate, b, c, states):
-    steps, seqs, width = x.shape
-    heads, state, rows = dt.shape[2], b.shape[2], steps * seqs
+def decode_scratch(arrays):
+    steps, seqs, width = arrays[4].shape
+    rows, state, heads = steps * seqs, arrays[6].shape[2], arrays[3].shape[2]
+    wide, narrow, small = (pltpu.VMEM((rows, n), F32) for n in (width, state, heads))
+    return [
+        *(pltpu.VMEM(a.shape, a.dtype) for a in arrays),
+        wide, wide, narrow, narrow, small, small, wide, wide,
+        pltpu.SemaphoreType.DMA((len(arrays),)),
+    ]
+
+
+def decode_own(turn, arrays):
+    steps, seqs, width = arrays[4].shape
+    state, rows = arrays[6].shape[2], steps * seqs
     return pl.pallas_call(
-        decode_kernel,
+        functools.partial(decode_kernel, turn),
         name="decode_own",
-        out_shape=[jax.ShapeDtypeStruct((rows, width), F32)] * 2,
-        grid=(seqs,),
-        in_specs=[
-            SMEM, whole((1, heads)), whole((1, heads)), whole((steps, seqs, heads)),
-            whole((steps, seqs, width)), whole((steps, seqs, width)),
-            whole((steps, seqs, state)), whole((steps, seqs, state)),
-            by_rows((1, width, state)),
-        ],
-        out_specs=[whole((rows, width))] * 2,
-        scratch_shapes=[
-            pltpu.VMEM((rows, width), F32), pltpu.VMEM((rows, width), F32),
-            pltpu.VMEM((rows, state), F32), pltpu.VMEM((rows, state), F32),
-            pltpu.VMEM((rows, heads), F32), pltpu.VMEM((rows, heads), F32),
-        ],
-        compiler_params=params(16),
+        out_shape=[pltpu.HBM((rows, width), F32)] * 2,
+        in_specs=[HBM] * len(arrays),
+        out_specs=[HBM] * 2,
+        scratch_shapes=[*decode_scratch(arrays), pltpu.SemaphoreType.DMA((2,))],
+        compiler_params=pltpu.CompilerParams(vmem_limit_bytes=32 * 2**20),
         cost_estimate=cost(4 * seqs * 256 * state * width, 5),
-    )(slots, *map(in_hbm, (rate, skip, dt, x, gate, b, c, states)))
+    )(*map(in_hbm, arrays))
 
 
 def prefix(owned):
@@ -445,24 +499,26 @@
     )(owned)
 
 
-def mix(coef, slots, entry, c, part, dec_part, dec_coef):
+def mix(turn, decode, coef, dec_part, dec_coef, slots, entry, c, part):
     length, width = part.shape
     return pl.pallas_call(
-        mix_kernel,
+        functools.partial(mix_kernel, turn),
         name="mix",
         out_shape=[
             pltpu.VMEM((length, width), F32),
             pltpu.VMEM(dec_part.shape, F32),
             pltpu.VMEM((8, SPAN), F32),
         ],
-        in_specs=[HBM] + [VMEM] * 6,
+        in_specs=[HBM] * 12 + [VMEM] * 4,
         out_specs=[VMEM] * 3,
         scratch_shapes=[
-            pltpu.VMEM((length, width), F32), pltpu.SemaphoreType.DMA((length // SPAN,)),
+            pltpu.VMEM((length, width), F32),
+            pltpu.SemaphoreType.DMA((length // SPAN + 2,)),
+            *decode_scratch(decode),
         ],
-        compiler_params=pltpu.CompilerParams(vmem_limit_bytes=32 * 2**20),
+        compiler_params=pltpu.CompilerParams(vmem_limit_bytes=40 * 2**20),
         cost_estimate=cost(4 * length * c.shape[1] * width, 14),
-    )(in_hbm(coef), slots, entry, c, part, dec_part, dec_coef)
+    )(*map(in_hbm, (*decode, coef, dec_part, dec_coef)), slots, entry, c, part)
 
 
 def norm(power, other, gain, mixed, dec_mixed, dec_shape):
@@ -499,18 +555,19 @@
     dec_dt = dec_dt.reshape(steps, seqs, heads)
 
     slots_row = slots.reshape(1, seqs)
-    sent = device_state(lengths, decay_rate, slots_row, dt, x, b, dec_c, count)
+    decode = (
+        slots_row, decay_rate, skip_gain, dec_dt, dec_x, dec_gate, dec_b, dec_c,
+        dec_states.reshape(seqs, width, state),
+    )
+    dec_part, dec_coef = decode_own(0, decode)
+    sent = device_state(lengths, decay_rate, slots_row, dt, x, b, dec_c, dec_part, count)
     owned = lax.all_to_all(sent, SEQ, 0, 0)
     part, coef = device_outputs(lengths, decay_rate, skip_gain, dt, x, gate, b, c)
-    dec_part, dec_coef = decode_own(
-        slots, decay_rate, skip_gain, dec_dt, dec_x, dec_gate, dec_b, dec_c,
-        dec_states.reshape(seqs, width, state),
-    )
-    owned, part, coef, dec_part, dec_coef = lax.optimization_barrier(
-        (owned, part, coef, dec_part, dec_coef)
-    )
+    owned, part, coef = lax.optimization_barrier((owned, part, coef))
     entry = lax.all_to_all(prefix(owned), SEQ, 0, 0)
-    mixed, dec_mixed, power = mix(coef, slots_row, entry, c, part, dec_part, dec_coef)
+    mixed, dec_mixed, power = mix(
+        1, decode, coef, dec_part, dec_coef, slots_row, entry, c, part
+    )
     other = lax.ppermute(power, "pool", [(0, 1), (1, 0)])
     prefill_out, decode_out = norm(
         power, other, norm_gain, mixed, dec_mixed, (steps, seqs, width)

time: 63.3 us -> 59.6 us (0.942)
  blocking collectives: 21.2 us -> 17.2 us
    all_to_all x1, blocking collectives: 21.2 us -> 17.2 us  [shards(): entry = lax.all_to_all(prefix(owned), SEQ, 0, 0)]
  transfers between devices with their start and end apart: 2 -> 2, of which waited for: 2 -> 2; matrix products, arithmetic and copies ran while one was open for 0% -> 0% of each run, Pallas kernels for 26% -> 19%
where the time goes in v3:
time: 59.6 us; the launch traced here: 59.3 us
  Pallas kernels  26.2 us (44%)
  blocking collectives  17.2 us (29%)
  starting transfers between devices  11.4 us (19%)
  waiting for transfers between devices  3.12 us (5%)
  between operations  1.32 us (2%)
    all_to_all x1, blocking collectives, shards(): entry = lax.all_to_all(prefix(owned), SEQ, 0, 0)  17.2 us
    pallas_call x1, Pallas kernels, device_outputs(): pl.pallas_call(local_kernel, name='device_outputs', out_shape=[pltpu.HBM(...  11.5 us
    pallas_call x1, Pallas kernels, mix(): pl.pallas_call(functools.partial(mix_kernel, turn), name='mix', out_shape...  7.83 us
    all_to_all x1, starting transfers between devices, shards(): owned = lax.all_to_all(sent, SEQ, 0, 0)  7.59 us
    pallas_call x1, Pallas kernels, device_state(): pl.pallas_call(state_kernel, name='device_state', out_shape=pltpu.HBM(sha...  4.34 us
    ppermute x1, starting transfers between devices, shards(): other = lax.ppermute(power, 'pool', [(0, 1), (1, 0)])  3.79 us
    all_to_all x1, waiting for transfers between devices, shards(): owned = lax.all_to_all(sent, SEQ, 0, 0)  2.29 us
    pallas_call x1, Pallas kernels, norm(): pl.pallas_call(norm_kernel, name='norm', out_shape=[pltpu.HBM((length, wi...  2.16 us
  transfers between devices with their start and end apart: 2, of which 2 were waited for; matrix products, arithmetic and copies ran while one was open for 0% of the time, Pallas kernels for 19%

profile of v3, /device:TPU:1, one launch (start us, length us, event | category | flops | bytes accessed | tf_op | source)
XLA Modules:
  0.0 59.3 jit_solution(17712291277888410506)
XLA Ops:
  1.3 0.1 decode_own.1
  1.4 4.3 %device_state.1 = f32[16,160,128]{2,1,0:T(8,128)} custom-call(s32[1]{0:T(128)S(6)} %copy.19.lengths_ref, f32[1,16]{1,0:T(1,128)} %refs_1_.3, s32[1,4]{1,0:T(1,128)} %bitcast.34, bf16[16,1024]{1,0:T(8,128)(2,1)} %bitcast.44, bf16[1024,1024]{1,0:T(8,128)(2,1)} %bitcast.37, bf16[1024,256]{1,0:T(8,128)(2,1)} %bitcast.41, bf16[8,4,256]{2,1,0:T(4,128)(2,1)} %bitcast.29, ...), custom_call_target="tpu_custom_call" | custom-call | flops 2147483648 | bytes 6291456 | tf_op jit(solution)/shard_map/device_state/pallas_call | solution.py:417
  5.8 7.6 %all-to-all-start = ((f32[16,160,128]{2,1,0:T(8,128)}), f32[16,160,128]{2,1,0:T(8,128)S(1)}, u32[]{:S(2)}, u32[]{:S(2)}) async-start(f32[16,160,128]{2,1,0:T(8,128)} %device_state.1), calls=%async_computation | async-start | bytes 2621440 | tf_op jit(solution)/shard_map/all_to_all | solution.py:564
  13.4 11.5 %device_outputs.1 = (f32[1024,1024]{1,0:T(8,128)}, f32[1024,1024]{1,0:T(8,128)}) custom-call(s32[1]{0:T(128)S(6)} %copy.19.lengths_ref, f32[1,16]{1,0:T(1,128)} %refs_1_.3, f32[1,16]{1,0:T(1,128)} %refs_2_.3, bf16[16,1024]{1,0:T(8,128)(2,1)} %bitcast.45, bf16[1024,1024]{1,0:T(8,128)(2,1)} %bitcast.38, bf16[1024,1024]{1,0:T(8,128)(2,1)} %bitcast.39, ...), custom_call_target="tpu_custom_call" | custom-call | flops 5368709120 | bytes 14680064 | tf_op jit(solution)/shard_map/device_outputs/pallas_call | solution.py:445
  24.9 2.3 %all-to-all-done.in_ref = f32[16,160,128]{2,1,0:T(8,128)S(1)} async-done(((f32[16,160,128]{2,1,0:T(8,128)}), f32[16,160,128]{2,1,0:T(8,128)S(1)}, u32[]{:S(2)}, u32[]{:S(2)}) %all-to-all-start) | async-done | bytes 1310752 | tf_op jit(solution)/shard_map/all_to_all | solution.py:564
  27.2 0.0 copy-start
  27.2 0.0 copy-start.1
  27.2 0.3 prefix.1
  27.4 17.2 %all_to_all.10.refs_13_ = f32[16,152,128]{2,1,0:T(8,128)S(1)} all-to-all(f32[16,152,128]{2,1,0:T(8,128)S(1)} %prefix.1), channel_id=1, replica_groups=mesh['pool'=2,'seq_0'=4,'seq_1'=4,'head'=8] {'seq_0','seq_1'}, dimensions={0} | all-to-all | bytes 2490368 | tf_op jit(solution)/shard_map/all_to_all | solution.py:567
  44.7 0.0 copy-done
  44.7 0.0 copy-done.1
  44.7 0.0 copy-start.2
  44.7 7.8 %mix.1 = (f32[1024,1024]{1,0:T(8,128)S(1)}, f32[32,1024]{1,0:T(8,128)S(1)}, f32[8,256]{1,0:T(8,128)S(1)}) custom-call(s32[1,4]{1,0:T(1,128)} %bitcast.35, f32[1,16]{1,0:T(1,128)} %refs_1_.3, f32[1,16]{1,0:T(1,128)} %refs_2_.3, bf16[8,4,16]{2,1,0:T(4,128)(2,1)} %bitcast.32, bf16[8,4,1024]{2,1,0:T(4,128)(2,1)} %bitcast.23, bf16[8,4,1024]{2,1,0:T(4,128)(2,1)} %bitcast.25, ...), custom_call_target="tpu_custom_call" | custom-call | flops 1073741824 | bytes 14680064 | tf_op jit(solution)/shard_map/mix/pallas_call | solution.py:504
  52.5 3.8 %collective-permute-start = (f32[8,256]{1,0:T(8,128)S(1)}, f32[8,256]{1,0:T(8,128)S(1)}, u32[]{:S(2)}, u32[]{:S(2)}) collective-permute-start(f32[8,256]{1,0:T(8,128)S(1)} %get-tuple-element.21.power_ref), channel_id=1, source_target_pairs={{0,128},{128,0},{1,129},{129,1},{2,130},{130,2},{3,131},{131,3},{4... | collective-permute-start | bytes 24584 | tf_op jit(solution)/shard_map/ppermute | solution.py:571
  56.3 0.8 %collective-permute-done.other_ref = f32[8,256]{1,0:T(8,128)S(1)} collective-permute-done((f32[8,256]{1,0:T(8,128)S(1)}, f32[8,256]{1,0:T(8,128)S(1)}, u32[]{:S(2)}, u32[]{:S(2)}) %collective-permute-start) | collective-permute-done | bytes 8224 | tf_op jit(solution)/shard_map/ppermute | solution.py:571
  57.2 0.0 copy-done.2
  57.2 2.2 %norm.1 = (bf16[1024,1024]{1,0:T(8,128)(2,1)}, bf16[8,4,1024]{2,1,0:T(4,128)(2,1)}) custom-call(f32[8,256]{1,0:T(8,128)S(1)} %get-tuple-element.21.power_ref, f32[8,256]{1,0:T(8,128)S(1)} %collective-permute-done.other_ref, f32[1,1024]{1,0:T(1,128)S(1)} %copy-done.2, f32[1024,1024]{1,0:T(8,128)S(1)} %get-tuple-element.22.mixed_ref, ...), custom_call_target="tpu_custom_call" | custom-call | flops 4194304 | bytes 6291456 | tf_op jit(solution)/shard_map/norm/pallas_call | solution.py:526
Async XLA Ops:
  5.8 21.4 %all-to-all-start = ((f32[16,160,128]{2,1,0:T(8,128)}), f32[16,160,128]{2,1,0:T(8,128)S(1)}, u32[]{:S(2)}, u32[]{:S(2)}) async-start(f32[16,160,128]{2,1,0:T(8,128)} %device_state.1), calls=%async_computation | async-start | bytes 2621440 | tf_op jit(solution)/shard_map/all_to_all | solution.py:564
  27.2 17.5 %copy-start = (f32[1024,1024]{1,0:T(8,128)S(1)}, f32[1024,1024]{1,0:T(8,128)}, u32[]{:S(2)}) copy-start(f32[1024,1024]{1,0:T(8,128)} %get-tuple-element.20.refs_15_) | copy-start | bytes 12582916
  27.2 17.5 %copy-start.1 = (bf16[1,1024,1,256]{3,1,2,0:T(8,128)(2,1)S(1)}, bf16[1,1024,1,256]{3,1,2,0:T(8,128)(2,1)}, u32[]{:S(2)}) copy-start(bf16[1,1024,1,256]{3,1,2,0:T(8,128)(2,1)} %param.20) | copy-start | bytes 1572868
  44.7 12.5 %copy-start.2 = (f32[1,1024]{1,0:T(1,128)S(1)}, f32[1,1024]{1,0:T(1,128)}, u32[]{:S(2)}) copy-start(f32[1,1024]{1,0:T(1,128)} %gain_ref.1) | copy-start | bytes 12292
  52.5 4.6 %collective-permute-start = (f32[8,256]{1,0:T(8,128)S(1)}, f32[8,256]{1,0:T(8,128)S(1)}, u32[]{:S(2)}, u32[]{:S(2)}) collective-permute-start(f32[8,256]{1,0:T(8,128)S(1)} %get-tuple-element.21.power_ref), channel_id=1, source_target_pairs={{0,128},{128,0},{1,129},{129,1},{2,130},{130,2},{3,131},{131,3},{4... | collective-permute-start | bytes 24584 | tf_op jit(solution)/shard_map/ppermute | solution.py:571

commit v4 on v3

--- a/solution.py
+++ b/solution.py
@@ -249,12 +249,12 @@
     pairs = (
         (slots_hbm, slots_ref), (rate_hbm, rate_ref), (skip_hbm, skip_ref), (dt_hbm, dt_ref),
         (x_hbm, x_ref), (gate_hbm, gate_ref), (b_hbm, b_ref), (c_hbm, c_ref),
-        (states_hbm, states),
+        *((states_hbm.at[d], states.at[d]) for d in range(states.shape[0])),
     )
     loads = [pltpu.make_async_copy(*pair, sem.at[n]) for n, pair in enumerate(pairs)]
     for load in loads:
         load.start()
-    for load in loads[:-1]:
+    for load in loads[:-seqs]:
         load.wait()
     total = jnp.zeros((seqs, heads), F32)
     for s in range(steps):
@@ -278,10 +278,10 @@
     skip = exact_dot(jnp.broadcast_to(skip_ref[...], (8, heads)), table)[0:1]
     gate = silu(gate_all[...])
     seq = iota((rows, 1), 0) % seqs
-    loads[-1].wait()
     own = jnp.zeros((rows, width), F32)
     keeps = jnp.zeros((rows, 1), jnp.int32)
     for d in range(seqs):
+        loads[d - seqs].wait()
         high, low = split2(states[d])
         mine = (seq == d) & (slots_ref[:, d : d + 1] < 0)
         own = jnp.where(mine, dot(c, high, 1, 1) + dot(c, low, 1, 1), own)
@@ -469,7 +469,7 @@
     return [
         *(pltpu.VMEM(a.shape, a.dtype) for a in arrays),
         wide, wide, narrow, narrow, small, small, wide, wide,
-        pltpu.SemaphoreType.DMA((len(arrays),)),
+        pltpu.SemaphoreType.DMA((len(arrays) + arrays[8].shape[0],)),
     ]
 
 

time: 59.6 us -> 59.6 us (level)
  no operation moved by 1% of the time
where the time goes in v4:
time: 59.6 us; the launch traced here: 59.3 us
  Pallas kernels  25.7 us (43%)
  blocking collectives  17.2 us (29%)
  starting transfers between devices  11.7 us (20%)
  waiting for transfers between devices  3.36 us (6%)
  between operations  1.32 us (2%)
    all_to_all x1, blocking collectives, shards(): entry = lax.all_to_all(prefix(owned), SEQ, 0, 0)  17.2 us
    pallas_call x1, Pallas kernels, device_outputs(): pl.pallas_call(local_kernel, name='device_outputs', out_shape=[pltpu.HBM(...  11.5 us
    all_to_all x1, starting transfers between devices, shards(): owned = lax.all_to_all(sent, SEQ, 0, 0)  7.6 us
    pallas_call x1, Pallas kernels, mix(): pl.pallas_call(functools.partial(mix_kernel, turn), name='mix', out_shape...  7.25 us
    pallas_call x1, Pallas kernels, device_state(): pl.pallas_call(state_kernel, name='device_state', out_shape=pltpu.HBM(sha...  4.34 us
    ppermute x1, starting transfers between devices, shards(): other = lax.ppermute(power, 'pool', [(0, 1), (1, 0)])  4.15 us
    all_to_all x1, waiting for transfers between devices, shards(): owned = lax.all_to_all(sent, SEQ, 0, 0)  2.53 us
    pallas_call x1, Pallas kernels, norm(): pl.pallas_call(norm_kernel, name='norm', out_shape=[pltpu.HBM((length, wi...  2.16 us
  transfers between devices with their start and end apart: 2, of which 2 were waited for; matrix products, arithmetic and copies ran while one was open for 0% of the time, Pallas kernels for 19%

profile of v4, /device:TPU:1, one launch (start us, length us, event | category | flops | bytes accessed | tf_op | source)
XLA Modules:
  0.0 59.3 jit_solution(11474066798873276230)
XLA Ops:
  1.3 0.2 decode_own.1
  1.4 4.3 %device_state.1 = f32[16,160,128]{2,1,0:T(8,128)} custom-call(s32[1]{0:T(128)S(6)} %copy.19.lengths_ref, f32[1,16]{1,0:T(1,128)} %refs_1_.3, s32[1,4]{1,0:T(1,128)} %bitcast.34, bf16[16,1024]{1,0:T(8,128)(2,1)} %bitcast.44, bf16[1024,1024]{1,0:T(8,128)(2,1)} %bitcast.37, bf16[1024,256]{1,0:T(8,128)(2,1)} %bitcast.41, bf16[8,4,256]{2,1,0:T(4,128)(2,1)} %bitcast.29, ...), custom_call_target="tpu_custom_call" | custom-call | flops 2147483648 | bytes 6291456 | tf_op jit(solution)/shard_map/device_state/pallas_call | solution.py:417
  5.8 7.6 %all-to-all-start = ((f32[16,160,128]{2,1,0:T(8,128)}), f32[16,160,128]{2,1,0:T(8,128)S(1)}, u32[]{:S(2)}, u32[]{:S(2)}) async-start(f32[16,160,128]{2,1,0:T(8,128)} %device_state.1), calls=%async_computation | async-start | bytes 2621440 | tf_op jit(solution)/shard_map/all_to_all | solution.py:564
  13.4 11.5 %device_outputs.1 = (f32[1024,1024]{1,0:T(8,128)}, f32[1024,1024]{1,0:T(8,128)}) custom-call(s32[1]{0:T(128)S(6)} %copy.19.lengths_ref, f32[1,16]{1,0:T(1,128)} %refs_1_.3, f32[1,16]{1,0:T(1,128)} %refs_2_.3, bf16[16,1024]{1,0:T(8,128)(2,1)} %bitcast.45, bf16[1024,1024]{1,0:T(8,128)(2,1)} %bitcast.38, bf16[1024,1024]{1,0:T(8,128)(2,1)} %bitcast.39, ...), custom_call_target="tpu_custom_call" | custom-call | flops 5368709120 | bytes 14680064 | tf_op jit(solution)/shard_map/device_outputs/pallas_call | solution.py:445
  24.9 2.5 %all-to-all-done.in_ref = f32[16,160,128]{2,1,0:T(8,128)S(1)} async-done(((f32[16,160,128]{2,1,0:T(8,128)}), f32[16,160,128]{2,1,0:T(8,128)S(1)}, u32[]{:S(2)}, u32[]{:S(2)}) %all-to-all-start) | async-done | bytes 1310752 | tf_op jit(solution)/shard_map/all_to_all | solution.py:564
  27.4 0.0 copy-start
  27.4 0.0 copy-start.1
  27.4 0.3 prefix.1
  27.7 17.2 %all_to_all.10.refs_13_ = f32[16,152,128]{2,1,0:T(8,128)S(1)} all-to-all(f32[16,152,128]{2,1,0:T(8,128)S(1)} %prefix.1), channel_id=1, replica_groups=mesh['pool'=2,'seq_0'=4,'seq_1'=4,'head'=8] {'seq_0','seq_1'}, dimensions={0} | all-to-all | bytes 2490368 | tf_op jit(solution)/shard_map/all_to_all | solution.py:567
  44.9 0.0 copy-done
  44.9 0.0 copy-done.1
  44.9 0.0 copy-start.2
  44.9 7.3 %mix.1 = (f32[1024,1024]{1,0:T(8,128)S(1)}, f32[32,1024]{1,0:T(8,128)S(1)}, f32[8,256]{1,0:T(8,128)S(1)}) custom-call(s32[1,4]{1,0:T(1,128)} %bitcast.35, f32[1,16]{1,0:T(1,128)} %refs_1_.3, f32[1,16]{1,0:T(1,128)} %refs_2_.3, bf16[8,4,16]{2,1,0:T(4,128)(2,1)} %bitcast.32, bf16[8,4,1024]{2,1,0:T(4,128)(2,1)} %bitcast.23, bf16[8,4,1024]{2,1,0:T(4,128)(2,1)} %bitcast.25, ...), custom_call_target="tpu_custom_call" | custom-call | flops 1073741824 | bytes 14680064 | tf_op jit(solution)/shard_map/mix/pallas_call | solution.py:504
  52.2 4.1 %collective-permute-start = (f32[8,256]{1,0:T(8,128)S(1)}, f32[8,256]{1,0:T(8,128)S(1)}, u32[]{:S(2)}, u32[]{:S(2)}) collective-permute-start(f32[8,256]{1,0:T(8,128)S(1)} %get-tuple-element.21.power_ref), channel_id=1, source_target_pairs={{0,128},{128,0},{1,129},{129,1},{2,130},{130,2},{3,131},{131,3},{4... | collective-permute-start | bytes 24584 | tf_op jit(solution)/shard_map/ppermute | solution.py:571
  56.3 0.8 %collective-permute-done.other_ref = f32[8,256]{1,0:T(8,128)S(1)} collective-permute-done((f32[8,256]{1,0:T(8,128)S(1)}, f32[8,256]{1,0:T(8,128)S(1)}, u32[]{:S(2)}, u32[]{:S(2)}) %collective-permute-start) | collective-permute-done | bytes 8224 | tf_op jit(solution)/shard_map/ppermute | solution.py:571
  57.2 0.0 copy-done.2
  57.2 2.2 %norm.1 = (bf16[1024,1024]{1,0:T(8,128)(2,1)}, bf16[8,4,1024]{2,1,0:T(4,128)(2,1)}) custom-call(f32[8,256]{1,0:T(8,128)S(1)} %get-tuple-element.21.power_ref, f32[8,256]{1,0:T(8,128)S(1)} %collective-permute-done.other_ref, f32[1,1024]{1,0:T(1,128)S(1)} %copy-done.2, f32[1024,1024]{1,0:T(8,128)S(1)} %get-tuple-element.22.mixed_ref, ...), custom_call_target="tpu_custom_call" | custom-call | flops 4194304 | bytes 6291456 | tf_op jit(solution)/shard_map/norm/pallas_call | solution.py:526
Async XLA Ops:
  5.8 21.7 %all-to-all-start = ((f32[16,160,128]{2,1,0:T(8,128)}), f32[16,160,128]{2,1,0:T(8,128)S(1)}, u32[]{:S(2)}, u32[]{:S(2)}) async-start(f32[16,160,128]{2,1,0:T(8,128)} %device_state.1), calls=%async_computation | async-start | bytes 2621440 | tf_op jit(solution)/shard_map/all_to_all | solution.py:564
  27.4 17.5 %copy-start = (f32[1024,1024]{1,0:T(8,128)S(1)}, f32[1024,1024]{1,0:T(8,128)}, u32[]{:S(2)}) copy-start(f32[1024,1024]{1,0:T(8,128)} %get-tuple-element.20.refs_15_) | copy-start | bytes 12582916
  27.4 17.5 %copy-start.1 = (bf16[1,1024,1,256]{3,1,2,0:T(8,128)(2,1)S(1)}, bf16[1,1024,1,256]{3,1,2,0:T(8,128)(2,1)}, u32[]{:S(2)}) copy-start(bf16[1,1024,1,256]{3,1,2,0:T(8,128)(2,1)} %param.20) | copy-start | bytes 1572868
  44.9 12.2 %copy-start.2 = (f32[1,1024]{1,0:T(1,128)S(1)}, f32[1,1024]{1,0:T(1,128)}, u32[]{:S(2)}) copy-start(f32[1,1024]{1,0:T(1,128)} %gain_ref.1) | copy-start | bytes 12292
  52.2 5.0 %collective-permute-start = (f32[8,256]{1,0:T(8,128)S(1)}, f32[8,256]{1,0:T(8,128)S(1)}, u32[]{:S(2)}, u32[]{:S(2)}) collective-permute-start(f32[8,256]{1,0:T(8,128)S(1)} %get-tuple-element.21.power_ref), channel_id=1, source_target_pairs={{0,128},{128,0},{1,129},{129,1},{2,130},{130,2},{3,131},{131,3},{4... | collective-permute-start | bytes 24584 | tf_op jit(solution)/shard_map/ppermute | solution.py:571
